TPU v7x, 256 devices: a whole 4x4x8 slice. The times are simulated.
256 devices in a mesh: dp: 16 (over z, core), expert: 16 (over y, x).
Axes of the slice: x: 4, y: 4, z: 8, core: 2. Of those that a mesh axis runs over, the one named last changes fastest.
Arguments:
- gen_rows: bfloat16 [32768, 2048], P(('dp', 'expert')), may hold values from -6 to 6
- gen_lengths: int32 [16, 16, 8], P('dp', 'expert'), may hold values from 1 to 16, as said below
- gen_adv: bfloat16 [16, 16, 8], P('dp', 'expert'), may hold values from -4 to 4
- destination: int32 [16, 16, 8], P('dp', 'expert'), may hold values from 0 to 15, as said below
- expert_ids: int32 [32768, 2], P(('dp', 'expert')), may hold values from 0 to 15, all different within a row; in each aligned block of 128 rows (0 to 127, 128 to 255, ...) at most 32 rows name the same one
- gate_values: float32 [32768, 2], P(('dp', 'expert')), may hold values from 0.1 to 1
- cotangent: bfloat16 [32768, 2048], P(('dp', 'expert')), may hold values from -6 to 6
- w_gate: bfloat16 [16, 2048, 768], P('expert'), may hold values from -0.125 to 0.125
- w_up: bfloat16 [16, 2048, 768], P('expert'), may hold values from -0.125 to 0.125
- w_down: bfloat16 [16, 768, 2048], P('expert'), may hold values from -0.21875 to 0.21875
Outputs:
- layer_out: bfloat16 [32768, 2048], P(('dp', 'expert'))
- input_grad: bfloat16 [32768, 2048], P(('dp', 'expert'))
- grad_gate: bfloat16 [16, 2048, 768], P('expert', 'dp')
- grad_up: bfloat16 [16, 2048, 768], P('expert', 'dp')
- grad_down: bfloat16 [16, 768, 2048], P('expert', 'dp')
Inputs may be any that keep to these rules, and one draw needn't show every extreme that they name: `gen_lengths`: every device holds a sequence of exactly 16 tokens. `destination`: the sequences of one generation device go to distinct trainer ranks, and each trainer device receives exactly 8 sequences. `expert_ids`: within the rows of one device, no expert is named more than 32 times, a bound that some block reaches.
All inputs are finite; a program needn't handle non-finite values.
Results may differ from a plain program's by a relative error of at most 0.017.
Values may be sent and summed in bfloat16 or wider, within the bound.
A program may use at most 128 MiB of HBM per device.

v0:
```python
import functools

import jax
import jax.numpy as jnp
from jax import lax
from jax.sharding import PartitionSpec as P


def contract(left, right, left_dim, right_dim):
    return lax.dot_general(
        left, right, (((left_dim,), (right_dim,)), ((), ())), preferred_element_type=jnp.float32
    )


def on_device(
    gen_rows,
    gen_lengths,
    gen_adv,
    destination,
    expert_ids,
    gate_values,
    cotangent,
    w_gate,
    w_up,
    w_down,
):
    n_dp = lax.axis_size("dp")
    n_ex = lax.axis_size("expert")
    seq_dev = destination.shape[2]
    model_width = gen_rows.shape[1]
    slot_len = gen_rows.shape[0] // seq_dev
    per_token = expert_ids.shape[1]
    tok_rows = seq_dev * slot_len
    capacity = 2 * tok_rows * per_token // n_ex
    weight_gate = w_gate[0]
    weight_up = w_up[0]
    weight_down = w_down[0]
    hidden_units = weight_gate.shape[1]
    targets = destination[0, 0]
    bf = jnp.bfloat16
    peer_ids = jnp.arange(n_dp, dtype=jnp.int32)
    matches = targets[None, :] == peer_ids[:, None]
    same_place = jnp.arange(slot_len)[:, None] == jnp.arange(slot_len)[None, :]
    spread = (
        (matches[:, None, :, None] & same_place[None, :, None, :])
        .astype(bf)
        .reshape(n_dp * slot_len, tok_rows)
    )
    out_rows = jnp.dot(spread, gen_rows, preferred_element_type=jnp.float32).astype(bf)
    lens_adv = jnp.stack(
        [gen_lengths[0, 0].astype(jnp.float32), gen_adv[0, 0].astype(jnp.float32)], axis=0
    )
    out_meta = jnp.sum(jnp.where(matches[:, None, :], lens_adv[None], 0.0), axis=2)
    got_meta = lax.all_to_all(out_meta, "dp", split_axis=0, concat_axis=0, tiled=True)
    got_rows = lax.all_to_all(out_rows, "dp", split_axis=0, concat_axis=0, tiled=True)
    got_lengths, got_adv = got_meta[:, 0], got_meta[:, 1]
    arrived = got_lengths > 0
    earlier = peer_ids[None, :] < peer_ids[:, None]
    arrival = jnp.sum((earlier & arrived[None, :]).astype(jnp.int32), axis=1)
    chosen = arrived[None, :] & (arrival[None, :] == jnp.arange(seq_dev, dtype=jnp.int32)[:, None])
    place = (
        (chosen[:, None, :, None] & same_place[None, :, None, :])
        .astype(bf)
        .reshape(tok_rows, n_dp * slot_len)
    )
    seq_scale8 = jnp.where(arrived, got_adv / jnp.maximum(got_lengths, 1.0), 0.0)
    train_scale = jnp.sum(jnp.where(chosen, seq_scale8[None, :], 0.0), axis=1)
    train_lengths = jnp.sum(jnp.where(chosen, got_lengths[None, :], 0.0), axis=1)
    tok = jnp.arange(tok_rows, dtype=jnp.int32)
    position = (tok % slot_len).astype(jnp.float32)
    tok_len = jnp.repeat(train_lengths, slot_len)
    tok_scale = jnp.where(position < tok_len, jnp.repeat(train_scale, slot_len), 0.0)
    experts = jnp.arange(n_ex, dtype=jnp.int32)
    named = [expert_ids[:, k][None, :] == experts[:, None] for k in range(per_token)]
    routed = functools.reduce(jnp.logical_or, named)
    gate_of = sum(jnp.where(named[k], gate_values[:, k][None, :], 0.0) for k in range(per_token))
    before = (tok[:, None] < tok[None, :]).astype(bf)
    pos = jnp.dot(routed.astype(bf), before, preferred_element_type=jnp.float32)
    code = jnp.where(routed, pos, -1.0)
    buffer_rows = n_ex * capacity
    hit = code[:, None, :] == jnp.arange(capacity, dtype=jnp.float32)[None, :, None]
    pick = hit.astype(bf).reshape(buffer_rows, tok_rows)
    weighted = jnp.where(hit, gate_of[:, None, :], 0.0).reshape(buffer_rows, tok_rows)
    row_scale = jnp.sum(
        jnp.where(hit, (gate_of * tok_scale[None, :])[:, None, :], 0.0), axis=2
    ).reshape(buffer_rows, 1)
    send_dy = (
        (jnp.dot(pick, cotangent, preferred_element_type=jnp.float32) * row_scale)
        .astype(bf)
        .reshape(n_ex, capacity, model_width)
    )
    pick_got = jnp.dot(pick, place, preferred_element_type=jnp.float32).astype(bf)
    send_rows = (
        jnp.dot(pick_got, got_rows, preferred_element_type=jnp.float32)
        .astype(bf)
        .reshape(n_ex, capacity, model_width)
    )
    expert_in = lax.all_to_all(send_rows, "expert", split_axis=0, concat_axis=0, tiled=True)
    flat_in = expert_in.reshape(-1, model_width)
    gate_pre = jnp.dot(flat_in, weight_gate, preferred_element_type=jnp.float32)
    up_pre = jnp.dot(flat_in, weight_up, preferred_element_type=jnp.float32)
    hidden = (gate_pre * jax.nn.sigmoid(gate_pre) * up_pre).astype(jnp.bfloat16)
    outputs = (
        jnp.dot(hidden, weight_down, preferred_element_type=jnp.float32)
        .astype(jnp.bfloat16)
        .reshape(expert_in.shape)
    )
    returned = lax.all_to_all(outputs, "expert", split_axis=0, concat_axis=0, tiled=True)
    item_shape = (expert_in.shape[0], expert_in.shape[1], hidden_units)
    returned, expert_in, gate_all, up_all = (
        returned,
        expert_in,
        gate_pre.reshape(item_shape),
        up_pre.reshape(item_shape),
    )
    hi = weighted.astype(bf)
    lo = (weighted - hi.astype(jnp.float32)).astype(bf)
    flat_back = returned.reshape(buffer_rows, model_width)
    layer_out = (contract(hi, flat_back, 0, 0) + contract(lo, flat_back, 0, 0)).astype(bf)
    expert_dy = lax.all_to_all(send_dy, "expert", split_axis=0, concat_axis=0, tiled=True).reshape(
        -1, model_width
    )
    flat_in = expert_in.reshape(-1, model_width)
    gate_flat = gate_all.reshape(-1, hidden_units)
    up_flat = up_all.reshape(-1, hidden_units)
    sigmoid_g = jax.nn.sigmoid(gate_flat)
    activated = gate_flat * sigmoid_g
    hidden = (activated * up_flat).astype(jnp.bfloat16)
    hidden_grad = contract(expert_dy, weight_down, 1, 1)
    gate_grad = (hidden_grad * up_flat * sigmoid_g * (1.0 + gate_flat * (1.0 - sigmoid_g))).astype(
        jnp.bfloat16
    )
    up_grad = (hidden_grad * activated).astype(jnp.bfloat16)
    input_rows = (
        (contract(gate_grad, weight_gate, 1, 1) + contract(up_grad, weight_up, 1, 1))
        .astype(jnp.bfloat16)
        .reshape(n_ex, capacity, model_width)
    )
    back_rows = lax.all_to_all(input_rows, "expert", split_axis=0, concat_axis=0, tiled=True)
    input_grad = contract(pick, back_rows.reshape(buffer_rows, model_width), 0, 0).astype(bf)
    gate_sum, up_sum, down_sum = (
        lax.psum_scatter(
            contract(flat_in, gate_grad, 0, 0).astype(jnp.bfloat16),
            "dp",
            scatter_dimension=0,
            tiled=True,
        ).astype(jnp.float32),
        lax.psum_scatter(
            contract(flat_in, up_grad, 0, 0).astype(jnp.bfloat16),
            "dp",
            scatter_dimension=0,
            tiled=True,
        ).astype(jnp.float32),
        lax.psum_scatter(
            contract(hidden, expert_dy, 0, 0).astype(jnp.bfloat16),
            "dp",
            scatter_dimension=0,
            tiled=True,
        ).astype(jnp.float32),
    )
    return (
        layer_out,
        input_grad,
        gate_sum.astype(jnp.bfloat16)[None],
        up_sum.astype(jnp.bfloat16)[None],
        down_sum.astype(jnp.bfloat16)[None],
    )


def solution(mesh):
    in_specs = (
        P(("dp", "expert"), None),
        P("dp", "expert", None),
        P("dp", "expert", None),
        P("dp", "expert", None),
        P(("dp", "expert"), None),
        P(("dp", "expert"), None),
        P(("dp", "expert"), None),
        P("expert", None, None),
        P("expert", None, None),
        P("expert", None, None),
    )
    out_specs = (
        P(("dp", "expert"), None),
        P(("dp", "expert"), None),
        P("expert", "dp", None),
        P("expert", "dp", None),
        P("expert", "dp", None),
    )
    return jax.shard_map(
        on_device, mesh=mesh, in_specs=in_specs, out_specs=out_specs, check_vma=False
    )
```

profile of v0, /device:TPU:1, one launch (start us, length us, event | category | flops | bytes accessed | tf_op | source)
XLA Modules:
  0.0 340.7 jit_solution(6984824130908179725)
XLA Ops:
  7.2 0.8 convert_bitcast_fusion
  8.0 0.8 bitcast_convert_fusion
  8.8 0.7 iota_compare_fusion.9
  9.5 0.1 select_reduce_fusion.1
  9.6 0.7 copy.17
  10.3 10.0 %all-to-all-start = ((f32[16,1,2]{2,1,0:T(1,128)}), f32[16,1,2]{2,1,0:T(1,128)S(1)}, u32[]{:S(2)}, u32[]{:S(2)}) async-start(f32[16,1,2]{2,1,0:T(1,128)} %copy.17), calls=%async_computation | async-start | bytes 16384 | tf_op jit(solution)/shard_map/all_to_all | solution.py:54
  20.3 0.1 copy.19
  20.4 0.8 slice_bitcast_fusion.4
  21.1 0.2 broadcast_and_fusion
  21.3 0.4 and.83
  21.7 2.5 convolution_convert_fusion.4
  24.2 0.1 convolution_select_fusion
  24.4 0.1 bitcast_compare_fusion
  24.5 2.7 all-to-all-done
  27.2 4.7 %all-to-all-start.1 = ((bf16[16,16,2048]{2,1,0:T(8,128)(2,1)}), bf16[16,16,2048]{2,1,0:T(8,128)(2,1)}, u32[]{:S(2)}, u32[]{:S(2)}) async-start(bf16[16,16,2048]{2,1,0:T(8,128)(2,1)} %bitcast.101), calls=%async_computation.1 | async-start | bytes 2097152 | tf_op jit(solution)/shard_map/all_to_all | solution.py:55
  32.1 0.1 convert_reduce_fusion
  32.2 0.1 select_reduce_fusion.3
  32.4 0.1 reshape.401
  32.7 0.1 select_reduce_fusion
  32.9 3.1 multiply_convert_fusion
  36.0 24.1 %all-to-all-done.1 = bf16[16,16,2048]{2,1,0:T(8,128)(2,1)} async-done(((bf16[16,16,2048]{2,1,0:T(8,128)(2,1)}), bf16[16,16,2048]{2,1,0:T(8,128)(2,1)}, u32[]{:S(2)}, u32[]{:S(2)}) %all-to-all-start.1) | async-done | bytes 1048608 | tf_op jit(solution)/shard_map/all_to_all | solution.py:55
  60.1 6.8 %all-to-all-start.4 = ((bf16[16,32,2048]{2,1,0:T(8,128)(2,1)}), bf16[16,32,2048]{2,1,0:T(8,128)(2,1)}, u32[]{:S(2)}, u32[]{:S(2)}) async-start(bf16[16,32,2048]{2,1,0:T(8,128)(2,1)} %bitcast.99), calls=%async_computation.4 | async-start | bytes 4194304 | tf_op jit(solution)/shard_map/all_to_all | solution.py:120
  67.0 0.2 broadcast_and_fusion.1
  67.2 0.5 and.79
  67.6 3.4 %convolution_convert_fusion.3 = bf16[512,2048]{1,0:T(8,128)(2,1)} fusion(bf16[256,2048]{1,0:T(8,128)(2,1)} %bitcast.12, pred[512,128]{1,0:T(32,128)(4,1)S(1)} %bitcast.104, pred[128,256]{1,0:T(32,128)(4,1)S(1)} %and.79), kind=kOutput, calls=%fused_computation.17 | convolution fusion | flops 571604992 | bytes 3244032 | tf_op jit(solution)/shard_map/dot_general | solution.py:94
  71.1 29.2 %all-to-all-done.4 = bf16[16,32,2048]{2,1,0:T(8,128)(2,1)} async-done(((bf16[16,32,2048]{2,1,0:T(8,128)(2,1)}), bf16[16,32,2048]{2,1,0:T(8,128)(2,1)}, u32[]{:S(2)}, u32[]{:S(2)}) %all-to-all-start.4) | async-done | bytes 2097184 | tf_op jit(solution)/shard_map/all_to_all | solution.py:120
  100.3 4.4 %all-to-all-start.2 = ((bf16[16,32,2048]{2,1,0:T(8,128)(2,1)}), bf16[16,32,2048]{2,1,0:T(8,128)(2,1)}, u32[]{:S(2)}, u32[]{:S(2)}) async-start(bf16[16,32,2048]{2,1,0:T(8,128)(2,1)} %bitcast.100), calls=%async_computation.2 | async-start | bytes 4194304 | tf_op jit(solution)/shard_map/all_to_all | solution.py:98
  104.8 5.6 %fusion = f32[512,768]{1,0:T(8,128)} fusion(bf16[512,2048]{1,0:T(8,128)(2,1)} %bitcast.24, bf16[1,768,2048]{2,1,0:T(8,128)(2,1)} %param.19), kind=kOutput, calls=%fused_computation.5 | convolution fusion | flops 1610612736 | bytes 6815744 | tf_op jit(solution)/shard_map/dot_general | solution.py:10
  110.4 28.0 %all-to-all-done.2 = bf16[16,32,2048]{2,1,0:T(8,128)(2,1)} async-done(((bf16[16,32,2048]{2,1,0:T(8,128)(2,1)}), bf16[16,32,2048]{2,1,0:T(8,128)(2,1)}, u32[]{:S(2)}, u32[]{:S(2)}) %all-to-all-start.2) | async-done | bytes 2097184 | tf_op jit(solution)/shard_map/all_to_all | solution.py:98
  138.3 4.4 %fusion.6 = f32[512,768]{1,0:T(8,128)S(1)} fusion(bf16[512,2048]{1,0:T(8,128)(2,1)} %bitcast.14, bf16[1,2048,768]{2,1,0:T(8,128)(2,1)} %param.18), kind=kOutput, calls=%fused_computation.11 | convolution fusion | flops 1610612736 | bytes 6815744 | tf_op jit(solution)/shard_map/dot_general | solution.py:101
  142.8 5.1 %multiply_convert_fusion.2 = (bf16[512,768]{1,0:T(8,128)(2,1)}, bf16[512,768]{1,0:T(8,128)(2,1)}, bf16[512,768]{1,0:T(8,128)(2,1)S(1)}) fusion(f32[512,768]{1,0:T(8,128)S(1)} %copy-done.5, f32[512,768]{1,0:T(8,128)S(1)} %fusion.6, bf16[512,2048]{1,0:T(8,128)(2,1)} %bitcast.14, bf16[1,2048,768]{2,1,0:T(8,128)(2,1)S(1)} %copy-done), kind=kOutput, calls=%fused_computation.27 | convolution fusion | flops 1616510976 | bytes 10747904 | tf_op jit(solution)/shard_map/dot_general | solution.py:100
  147.9 0.9 copy-done.4
  148.8 5.1 %convolution_convert_fusion = bf16[768,2048]{1,0:T(8,128)(2,1)} fusion(bf16[512,768]{1,0:T(8,128)(2,1)S(1)} %get-tuple-element.9, bf16[512,2048]{1,0:T(8,128)(2,1)} %bitcast.24), kind=kOutput, calls=%fused_computation.2 | convolution fusion | flops 1612185600 | bytes 6029312 | tf_op jit(solution)/shard_map/dot_general | solution.py:10
  153.9 0.2 reduce-scatter.4.cloned.1.call-start
  154.1 5.3 %convolution_convert_fusion.2 = bf16[2048,768]{1,0:T(8,128)(2,1)} fusion(bf16[512,2048]{1,0:T(8,128)(2,1)} %bitcast.14, bf16[512,768]{1,0:T(8,128)(2,1)} %get-tuple-element.7), kind=kOutput, calls=%fused_computation.4 | convolution fusion | flops 1612185600 | bytes 6029312 | tf_op jit(solution)/shard_map/dot_general | solution.py:10
  159.5 5.3 %convolution_convert_fusion.1 = bf16[2048,768]{1,0:T(8,128)(2,1)} fusion(bf16[512,2048]{1,0:T(8,128)(2,1)} %bitcast.14, bf16[512,768]{1,0:T(8,128)(2,1)} %get-tuple-element.8), kind=kOutput, calls=%fused_computation.3 | convolution fusion | flops 1612185600 | bytes 6029312 | tf_op jit(solution)/shard_map/dot_general | solution.py:10
  164.9 5.4 %fusion.12 = bf16[512,2048]{1,0:T(8,128)(2,1)} fusion(bf16[512,768]{1,0:T(8,128)(2,1)} %copy-done.4, bf16[1,768,2048]{2,1,0:T(8,128)(2,1)} %param.19), kind=kOutput, calls=%fused_computation.18 | convolution fusion | flops 1611661312 | bytes 6029312 | tf_op jit(solution)/shard_map/dot_general | solution.py:104
  170.3 4.5 %all-to-all-start.3 = ((bf16[16,32,2048]{2,1,0:T(8,128)(2,1)}), bf16[16,32,2048]{2,1,0:T(8,128)(2,1)}, u32[]{:S(2)}, u32[]{:S(2)}) async-start(bf16[16,32,2048]{2,1,0:T(8,128)(2,1)} %bitcast.103), calls=%async_computation.3 | async-start | bytes 4194304 | tf_op jit(solution)/shard_map/all_to_all | solution.py:108
  174.8 4.0 %fusion.4 = f32[512,2048]{1,0:T(8,128)S(1)} fusion(bf16[512,768]{1,0:T(8,128)(2,1)} %get-tuple-element.8, bf16[1,2048,768]{2,1,0:T(8,128)(2,1)} %param.18), kind=kOutput, calls=%fused_computation.9 | convolution fusion | flops 1610612736 | bytes 8126464 | tf_op jit(solution)/shard_map/dot_general | solution.py:10
  178.8 3.1 add_convert_fusion
  181.9 23.9 %all-to-all-done.3 = bf16[16,32,2048]{2,1,0:T(8,128)(2,1)} async-done(((bf16[16,32,2048]{2,1,0:T(8,128)(2,1)}), bf16[16,32,2048]{2,1,0:T(8,128)(2,1)}, u32[]{:S(2)}, u32[]{:S(2)}) %all-to-all-start.3) | async-done | bytes 2097184 | tf_op jit(solution)/shard_map/all_to_all | solution.py:108
  205.8 4.4 %all-to-all-start.5 = ((bf16[16,32,2048]{2,1,0:T(8,128)(2,1)}), bf16[16,32,2048]{2,1,0:T(8,128)(2,1)}, u32[]{:S(2)}, u32[]{:S(2)}) async-start(bf16[16,32,2048]{2,1,0:T(8,128)(2,1)} %bitcast.102), calls=%async_computation.5 | async-start | bytes 4194304 | tf_op jit(solution)/shard_map/all_to_all | solution.py:139
  210.2 3.0 convolution_bitcast_fusion.1
  213.3 25.2 %all-to-all-done.5 = bf16[16,32,2048]{2,1,0:T(8,128)(2,1)} async-done(((bf16[16,32,2048]{2,1,0:T(8,128)(2,1)}), bf16[16,32,2048]{2,1,0:T(8,128)(2,1)}, u32[]{:S(2)}, u32[]{:S(2)}) %all-to-all-start.5) | async-done | bytes 2097184 | tf_op jit(solution)/shard_map/all_to_all | solution.py:139
  238.5 3.0 fusion.19
  241.5 2.9 fusion.18
  244.4 26.5 %reduce-scatter.4.cloned.1.call-done = bf16[128,768]{1,0:T(8,128)(2,1)} async-done(((bf16[2048,768]{1,0:T(8,128)(2,1)}), bf16[128,768]{1,0:T(8,128)(2,1)}) %reduce-scatter.4.cloned.1.call-update) | async-done | bytes 196624 | tf_op jit(solution)/shard_map/reduce_scatter | solution.py:142
  270.9 63.3 %reduce-scatter.6.cloned.1.call-done = bf16[128,768]{1,0:T(8,128)(2,1)} async-done(((bf16[2048,768]{1,0:T(8,128)(2,1)}), bf16[128,768]{1,0:T(8,128)(2,1)}) %reduce-scatter.6.cloned.1.call-update) | async-done | bytes 196624 | tf_op jit(solution)/shard_map/reduce_scatter | solution.py:148
  (34 shorter events, 0.7 us)
Async XLA Ops:
  7.2 135.6 %copy-start = (bf16[1,2048,768]{2,1,0:T(8,128)(2,1)S(1)}, bf16[1,2048,768]{2,1,0:T(8,128)(2,1)}, u32[]{:S(2)}) copy-start(bf16[1,2048,768]{2,1,0:T(8,128)(2,1)} %param.17) | copy-start | bytes 9437188
  10.3 16.9 %all-to-all-start = ((f32[16,1,2]{2,1,0:T(1,128)}), f32[16,1,2]{2,1,0:T(1,128)S(1)}, u32[]{:S(2)}, u32[]{:S(2)}) async-start(f32[16,1,2]{2,1,0:T(1,128)} %copy.17), calls=%async_computation | async-start | bytes 16384 | tf_op jit(solution)/shard_map/all_to_all | solution.py:54
  21.3 10.7 %copy-start.2 = (f32[128,2]{0,1:T(2,128)S(1)}, f32[128,2]{0,1:T(2,128)}, u32[]{:S(2)}) copy-start(f32[128,2]{0,1:T(2,128)} %param.15) | copy-start | bytes 3076
  27.2 32.9 %all-to-all-start.1 = ((bf16[16,16,2048]{2,1,0:T(8,128)(2,1)}), bf16[16,16,2048]{2,1,0:T(8,128)(2,1)}, u32[]{:S(2)}, u32[]{:S(2)}) async-start(bf16[16,16,2048]{2,1,0:T(8,128)(2,1)} %bitcast.101), calls=%async_computation.1 | async-start | bytes 2097152 | tf_op jit(solution)/shard_map/all_to_all | solution.py:55
  60.1 40.1 %all-to-all-start.4 = ((bf16[16,32,2048]{2,1,0:T(8,128)(2,1)}), bf16[16,32,2048]{2,1,0:T(8,128)(2,1)}, u32[]{:S(2)}, u32[]{:S(2)}) async-start(bf16[16,32,2048]{2,1,0:T(8,128)(2,1)} %bitcast.99), calls=%async_computation.4 | async-start | bytes 4194304 | tf_op jit(solution)/shard_map/all_to_all | solution.py:120
  100.3 38.1 %all-to-all-start.2 = ((bf16[16,32,2048]{2,1,0:T(8,128)(2,1)}), bf16[16,32,2048]{2,1,0:T(8,128)(2,1)}, u32[]{:S(2)}, u32[]{:S(2)}) async-start(bf16[16,32,2048]{2,1,0:T(8,128)(2,1)} %bitcast.100), calls=%async_computation.2 | async-start | bytes 4194304 | tf_op jit(solution)/shard_map/all_to_all | solution.py:98
  104.7 139.7 %reduce-scatter.8.cloned.1.call-start = ((), (), s32[]{:S(2)}) async-start(), calls=%async_computation.11 | async-start | bytes 3342336 | tf_op jit(solution)/shard_map/reduce_scatter | solution.py:154
  138.3 4.4 %copy-start.5 = (f32[512,768]{1,0:T(8,128)S(1)}, f32[512,768]{1,0:T(8,128)}, u32[]{:S(2)}) copy-start(f32[512,768]{1,0:T(8,128)} %fusion) | copy-start | bytes 4718596
  147.9 0.9 copy-start.4
  153.9 116.9 %reduce-scatter.4.cloned.1.call-start = ((), (), s32[]{:S(2)}) async-start(), calls=%async_computation.9 | async-start | bytes 3342336 | tf_op jit(solution)/shard_map/reduce_scatter | solution.py:142
  159.5 174.7 %reduce-scatter.6.cloned.1.call-start = ((), (), s32[]{:S(2)}) async-start(), calls=%async_computation.10 | async-start | bytes 3342336 | tf_op jit(solution)/shard_map/reduce_scatter | solution.py:148
  170.3 35.5 %all-to-all-start.3 = ((bf16[16,32,2048]{2,1,0:T(8,128)(2,1)}), bf16[16,32,2048]{2,1,0:T(8,128)(2,1)}, u32[]{:S(2)}, u32[]{:S(2)}) async-start(bf16[16,32,2048]{2,1,0:T(8,128)(2,1)} %bitcast.103), calls=%async_computation.3 | async-start | bytes 4194304 | tf_op jit(solution)/shard_map/all_to_all | solution.py:108
  174.7 4.0 %copy-start.3 = (bf16[512,768]{1,0:T(8,128)(2,1)S(1)}, bf16[512,768]{1,0:T(8,128)(2,1)}, u32[]{:S(2)}) copy-start(bf16[512,768]{1,0:T(8,128)(2,1)} %get-tuple-element.7) | copy-start | bytes 2359300
  205.8 32.7 %all-to-all-start.5 = ((bf16[16,32,2048]{2,1,0:T(8,128)(2,1)}), bf16[16,32,2048]{2,1,0:T(8,128)(2,1)}, u32[]{:S(2)}, u32[]{:S(2)}) async-start(bf16[16,32,2048]{2,1,0:T(8,128)(2,1)} %bitcast.102), calls=%async_computation.5 | async-start | bytes 4194304 | tf_op jit(solution)/shard_map/all_to_all | solution.py:139
  238.5 3.0 copy-start.1
Sparse Core Ops, SparseCore 0:
  154.0 53.5 reduce-scatter.7
  210.8 60.0 reduce-scatter.3
  274.0 60.1 reduce-scatter.5
where the time goes:
time: 343 us; the launch traced here: 341 us
  waiting for transfers between devices  223 us (65%)
  matrix products  61.4 us (18%)
  starting transfers between devices  35.1 us (10%)
  between operations  13.9 us (4%)
  local copies, waits for them, and re-layouts  3.86 us (1%)
  other arithmetic  3.45 us (1%)
    reduce_scatter x1, waiting for transfers between devices, on_device(): lax.psum_scatter(contract(flat_in, up_grad, 0, 0).astype(jnp.bfloat16), '...  63.3 us
    dot_general x9, matrix products, contract(): lax.dot_general(left, right, (((left_dim,), (right_dim,)), ((), ())), pre...  37.4 us
    all_to_all x1, waiting for transfers between devices, on_device(): lax.all_to_all(send_dy, 'expert', split_axis=0, concat_axis=0, tiled=True)  29.2 us
    all_to_all x1, waiting for transfers between devices, on_device(): lax.all_to_all(send_rows, 'expert', split_axis=0, concat_axis=0, tiled=True)  28 us
    reduce_scatter x1, waiting for transfers between devices, on_device(): lax.psum_scatter(contract(flat_in, gate_grad, 0, 0).astype(jnp.bfloat16),...  26.5 us
    all_to_all x1, waiting for transfers between devices, on_device(): lax.all_to_all(input_rows, 'expert', split_axis=0, concat_axis=0, tiled=T...  25.2 us
    all_to_all x1, waiting for transfers between devices, on_device(): lax.all_to_all(out_rows, 'dp', split_axis=0, concat_axis=0, tiled=True)  24.1 us
    all_to_all x1, waiting for transfers between devices, on_device(): lax.all_to_all(outputs, 'expert', split_axis=0, concat_axis=0, tiled=True)  23.9 us
  transfers between devices with their start and end apart: 9, of which 8 were waited for; matrix products, arithmetic and copies ran while one was open for 15% of the time, Pallas kernels for 0%

commit v1 on v0

v1 whole, which is shorter than its diff:
```python
import functools

import jax
import jax.numpy as jnp
from jax import lax
from jax.experimental import pallas as pl
from jax.experimental.pallas import tpu as pltpu
from jax.sharding import PartitionSpec as P

MESH = pl.DeviceIdType.MESH
BF = jnp.bfloat16
F32 = jnp.float32


def contract(left, right, left_dim, right_dim):
    return lax.dot_general(
        left, right, (((left_dim,), (right_dim,)), ((), ())), preferred_element_type=F32
    )


def iota(shape, dim):
    return lax.broadcasted_iota(jnp.int32, shape, dim)


def step_kernel(
    n_dp,
    n_ex,
    slot,
    cap,
    small_ref,
    gen_ref,
    cot_ref,
    wg_hbm,
    wu_hbm,
    wd_hbm,
    out_ref,
    dx_ref,
    gg_out,
    gu_out,
    gd_out,
    wg,
    wu,
    wd,
    meta_send,
    meta_recv,
    seq_send,
    seq_recv,
    x_send,
    x_recv,
    y_send,
    y_recv,
    o_send,
    o_recv,
    b_send,
    b_recv,
    pick,
    hi,
    lo,
    fac_a,
    fac_b,
    hid,
    gg,
    ug,
    grad_g,
    grad_u,
    grad_d,
    twin_g,
    twin_u,
    twin_d,
    ring_g,
    ring_u,
    ring_d,
    w_sem,
    meta_ss,
    meta_rs,
    seq_ss,
    seq_rs,
    x_ss,
    x_rs,
    y_ss,
    y_rs,
    o_ss,
    o_rs,
    b_ss,
    b_rs,
    twin_ss,
    twin_rs,
    ring_ss,
    ring_rs,
):
    g = lax.axis_index("dp")
    e = lax.axis_index("expert")
    core = lax.rem(g, 2)
    z = lax.div(g, 2)
    n_z = n_dp // 2
    half = n_z // 2
    rows = gen_ref.shape[0]
    width = gen_ref.shape[1]
    ff = wg.shape[1]
    slots = n_ex * cap
    dtile = min(256, width)
    ftile = min(256, ff)
    nd, nf = width // dtile, ff // ftile

    weights = [
        pltpu.make_async_copy(src, dst, w_sem.at[i])
        for i, (src, dst) in enumerate(((wg_hbm, wg), (wu_hbm, wu), (wd_hbm, wd)))
    ]
    for copy in weights:
        copy.start()

    barrier = pltpu.get_barrier_semaphore()

    @pl.loop(1, n_dp)
    def _(o):
        pl.semaphore_signal(barrier, 1, device_id={"dp": lax.rem(g + o, n_dp)}, device_id_type=MESH)

    @pl.loop(1, n_ex)
    def _(o):
        pl.semaphore_signal(
            barrier, 1, device_id={"expert": lax.rem(e + o, n_ex)}, device_id_type=MESH
        )

    shift = slot.bit_length() - 1
    dest_row = small_ref[0:1, :]
    len_row = small_ref[1:2, :]
    adv_row = small_ref[2:3, :]
    srow, scol = iota((n_dp * slot, rows), 0), iota((n_dp * slot, rows), 1)
    spread = (dest_row == (srow >> shift).astype(F32)) & ((srow & (slot - 1)) == (scol & (slot - 1)))
    spread = spread.astype(BF)
    mine = dest_row == iota((n_dp, rows), 0).astype(F32)
    first = (iota((n_dp, rows), 1) & (slot - 1)) == 0
    len_to = jnp.max(jnp.where(mine, len_row, 0.0), axis=1, keepdims=True)
    adv_to = jnp.sum(jnp.where(mine & first, adv_row, 0.0), axis=1, keepdims=True)
    line = iota((n_dp, 8, 128), 1)
    meta_send[...] = jnp.where(line == 0, len_to[:, :, None], adv_to[:, :, None])

    @pl.loop(0, nd)
    def _(j):
        cols = pl.ds(pl.multiple_of(j * dtile, dtile), dtile)
        seq_send[:, :, cols] = (
            jnp.dot(spread, gen_ref[:, cols], preferred_element_type=F32)
            .astype(BF)
            .reshape(n_dp, slot, dtile)
        )

    names = iota((n_ex, rows), 0).astype(F32)
    hit0, hit1 = small_ref[3:4, :] == names, small_ref[4:5, :] == names
    routed = hit0 | hit1
    gate_of = jnp.where(hit0, small_ref[5:6, :], 0.0) + jnp.where(hit1, small_ref[6:7, :], 0.0)
    before = (iota((rows, rows), 0) < iota((rows, rows), 1)).astype(BF)
    pos = jnp.dot(routed.astype(BF), before, preferred_element_type=F32)
    code = jnp.where(routed, pos, -1.0)
    hit = code[:, None, :] == iota((n_ex, cap, rows), 1).astype(F32)
    picked = hit.astype(BF).reshape(slots, rows)
    pick[...] = picked
    weighted = jnp.where(hit, gate_of[:, None, :], 0.0).reshape(slots, rows)
    whole = weighted.astype(BF)
    hi[...] = whole
    lo[...] = (weighted - whole.astype(F32)).astype(BF)

    pl.semaphore_wait(barrier, n_dp + n_ex - 2)

    def exchange(axis, me, n, send, recv, ss, rs):
        def copy(o):
            peer = lax.rem(me + o, n)
            return pltpu.make_async_remote_copy(
                src_ref=send.at[peer],
                dst_ref=recv.at[me],
                send_sem=ss.at[o],
                recv_sem=rs.at[o],
                device_id={axis: peer},
                device_id_type=MESH,
            )

        def own():
            return pltpu.make_async_copy(send.at[me], recv.at[me], ss.at[0])

        def start():
            own().start()

            @pl.loop(1, n)
            def _(o):
                copy(o).start()

        def wait_recv():
            own().wait()

            @pl.loop(1, n)
            def _(o):
                copy(o).wait_recv()

        def wait_send():
            @pl.loop(1, n)
            def _(o):
                copy(o).wait_send()

        return start, wait_recv, wait_send

    meta_start, meta_wait, meta_done = exchange("dp", g, n_dp, meta_send, meta_recv, meta_ss, meta_rs)
    seq_start, seq_wait, seq_done = exchange("dp", g, n_dp, seq_send, seq_recv, seq_ss, seq_rs)
    x_start, x_wait, x_done = exchange("expert", e, n_ex, x_send, x_recv, x_ss, x_rs)
    y_start, y_wait, y_done = exchange("expert", e, n_ex, y_send, y_recv, y_ss, y_rs)
    o_start, o_wait, o_done = exchange("expert", e, n_ex, o_send, o_recv, o_ss, o_rs)
    b_start, b_wait, b_done = exchange("expert", e, n_ex, b_send, b_recv, b_ss, b_rs)

    meta_start()
    seq_start()
    meta_wait()

    got_len = meta_recv[:, 0, :]
    got_adv = meta_recv[:, 1, :]
    alive = (got_len > 0.0).astype(BF)
    lower = (iota((n_dp, n_dp), 1) < iota((n_dp, n_dp), 0)).astype(BF)
    arrival = jnp.dot(lower, alive, preferred_element_type=F32)
    arrival = jnp.where(got_len > 0.0, arrival, -1.0)
    per_len = got_adv / jnp.maximum(got_len, 1.0)

    def widen(v):
        return jnp.broadcast_to(v[:, None, :rows], (n_dp, slot, rows)).reshape(n_dp * slot, rows)

    placed = (widen(arrival) == (scol >> shift).astype(F32)) & (
        (srow & (slot - 1)) == (scol & (slot - 1))
    )
    within = (srow & (slot - 1)).astype(F32) < widen(got_len)
    tok_scale = jnp.sum(
        jnp.where(placed & within, widen(per_len), 0.0), axis=0, keepdims=True
    )
    row_scale = jnp.sum(
        jnp.where(hit, (gate_of * tok_scale)[:, None, :], 0.0), axis=2, keepdims=True
    ).reshape(slots, 1)

    @pl.loop(0, nd)
    def _(j):
        cols = pl.ds(pl.multiple_of(j * dtile, dtile), dtile)
        rowsel = jnp.dot(pick[...], cot_ref[:, cols], preferred_element_type=F32)
        y_send[:, :, cols] = (rowsel * row_scale).astype(BF).reshape(n_ex, cap, dtile)

    y_start()
    fetch = contract(picked, placed.astype(BF), 1, 1).astype(BF)
    seq_wait()

    @pl.loop(0, nd)
    def _(j):
        cols = pl.ds(pl.multiple_of(j * dtile, dtile), dtile)
        source = seq_recv[:, :, cols].reshape(n_dp * slot, dtile)
        x_send[:, :, cols] = (
            jnp.dot(fetch, source, preferred_element_type=F32).astype(BF).reshape(n_ex, cap, dtile)
        )

    x_start()
    for copy in weights:
        copy.wait()
    x_wait()

    @pl.loop(0, nf)
    def _(j):
        cols = pl.ds(pl.multiple_of(j * ftile, ftile), ftile)
        x_all = x_recv[...].reshape(slots, width)
        gate_pre = jnp.dot(x_all, wg[:, cols], preferred_element_type=F32)
        up_pre = jnp.dot(x_all, wu[:, cols], preferred_element_type=F32)
        sig = jax.nn.sigmoid(gate_pre)
        act = gate_pre * sig
        hid[:, cols] = (act * up_pre).astype(BF)
        fac_a[:, cols] = up_pre * sig * (1.0 + gate_pre * (1.0 - sig))
        fac_b[:, cols] = act

    @pl.loop(0, nd)
    def _(j):
        cols = pl.ds(pl.multiple_of(j * dtile, dtile), dtile)
        o_send[:, :, cols] = (
            jnp.dot(hid[...], wd[:, cols], preferred_element_type=F32)
            .astype(BF)
            .reshape(n_ex, cap, dtile)
        )

    o_start()
    y_wait()

    @pl.loop(0, nf)
    def _(j):
        cols = pl.ds(pl.multiple_of(j * ftile, ftile), ftile)
        y_all = y_recv[...].reshape(slots, width)
        hidden_grad = contract(y_all, wd[cols, :], 1, 1)
        gg[:, cols] = (hidden_grad * fac_a[:, cols]).astype(BF)
        ug[:, cols] = (hidden_grad * fac_b[:, cols]).astype(BF)

    grads = ((grad_d, twin_d, ring_d, gd_out), (grad_g, twin_g, ring_g, gg_out), (grad_u, twin_u, ring_u, gu_out))

    def block(i, b, c):
        part = grads[i][1].shape[1]
        return pl.ds(pl.multiple_of((b * 2 + c) * part, part), part)

    def twin_copy(i, b):
        return pltpu.make_async_remote_copy(
            src_ref=grads[i][0].at[block(i, b, 1 - core)],
            dst_ref=grads[i][1].at[b],
            send_sem=twin_ss.at[i, b],
            recv_sem=twin_rs.at[i, b],
            device_id={"dp": g + 1 - 2 * core},
            device_id_type=MESH,
        )

    def ring_copy(i, way, s):
        grad, _, ring, _ = grads[i]
        mid = grad.shape[1] // 2
        if s == 0:
            b = lax.rem(z + half, n_z)
            cols = pl.ds(way * mid, mid)
        else:
            b = lax.rem(z + (half - s) * (1 - 2 * way) + n_z, n_z)
            cols = pl.ds(0, 2 * mid)
        return pltpu.make_async_remote_copy(
            src_ref=grad.at[block(i, b, core), cols],
            dst_ref=ring.at[way, s, :, cols],
            send_sem=ring_ss.at[i, way, s],
            recv_sem=ring_rs.at[i, way, s],
            device_id={"dp": lax.rem(g + 2 * (1 - 2 * way) + n_dp, n_dp)},
            device_id_type=MESH,
        )

    def ring_step(i, s):
        grad, twin, ring, _ = grads[i]
        mid = grad.shape[1] // 2
        if s == 0:
            b = lax.rem(z + half, n_z)
            here = block(i, b, core)
            twin_copy(i, b).wait_recv()
            grad[here, :] = (grad[here, :].astype(F32) + twin[b].astype(F32)).astype(BF)
            ring_copy(i, 0, 0).start()
            ring_copy(i, 1, 0).start()
            return
        for way in range(2):
            b = lax.rem(z + (half - s) * (1 - 2 * way) + n_z, n_z)
            here = block(i, b, core)
            twin_copy(i, b).wait_recv()
            ring_copy(i, way, s - 1).wait_recv()
            if s == 1:
                near, far = pl.ds(way * mid, mid), pl.ds((1 - way) * mid, mid)
                grad[here, near] = (
                    grad[here, near].astype(F32)
                    + twin[b, :, near].astype(F32)
                    + ring[way, 0, :, near].astype(F32)
                ).astype(BF)
                grad[here, far] = (
                    grad[here, far].astype(F32) + twin[b, :, far].astype(F32)
                ).astype(BF)
            else:
                grad[here, :] = (
                    grad[here, :].astype(F32)
                    + twin[b].astype(F32)
                    + ring[way, s - 1].astype(F32)
                ).astype(BF)
            ring_copy(i, way, s).start()

    def ring_last(i):
        grad, twin, ring, out = grads[i]
        twin_copy(i, z).wait_recv()
        ring_copy(i, 0, half - 1).wait_recv()
        ring_copy(i, 1, half - 1).wait_recv()
        here = block(i, z, core)
        out[...] = (
            grad[here, :].astype(F32)
            + twin[z].astype(F32)
            + ring[0, half - 1].astype(F32)
            + ring[1, half - 1].astype(F32)
        ).astype(BF)

    @pl.loop(0, nf * nd)
    def _(j):
        units = pl.ds(pl.multiple_of(lax.div(j, nd) * ftile, ftile), ftile)
        cols = pl.ds(pl.multiple_of(lax.rem(j, nd) * dtile, dtile), dtile)
        grad_d[units, cols] = contract(
            hid[:, units], y_recv[:, :, cols].reshape(slots, dtile), 0, 0
        ).astype(BF)

    @pl.loop(0, n_z)
    def _(k):
        twin_copy(0, lax.rem(z + half + k, n_z)).start()

    @pl.loop(0, nd)
    def _(j):
        cols = pl.ds(pl.multiple_of(j * dtile, dtile), dtile)
        b_send[:, :, cols] = (
            (contract(gg[...], wg[cols, :], 1, 1) + contract(ug[...], wu[cols, :], 1, 1))
            .astype(BF)
            .reshape(n_ex, cap, dtile)
        )

    b_start()
    ring_step(0, 0)

    pair = width // n_z

    @pl.loop(0, n_z)
    def _(k):
        b = lax.rem(z + half + k, n_z)
        cols = pl.ds(pl.multiple_of(b * pair, pair), pair)
        x_part = x_recv[:, :, cols].reshape(slots, pair)
        grad_g[cols, :] = contract(x_part, gg[...], 0, 0).astype(BF)
        grad_u[cols, :] = contract(x_part, ug[...], 0, 0).astype(BF)
        twin_copy(1, b).start()
        twin_copy(2, b).start()

    ring_step(1, 0)
    ring_step(2, 0)
    for s in range(1, half):
        for i in range(3):
            ring_step(i, s)

    o_wait()

    @pl.loop(0, nd)
    def _(j):
        cols = pl.ds(pl.multiple_of(j * dtile, dtile), dtile)
        back = o_recv[:, :, cols].reshape(slots, dtile)
        out_ref[:, cols] = (contract(hi[...], back, 0, 0) + contract(lo[...], back, 0, 0)).astype(BF)

    b_wait()

    @pl.loop(0, nd)
    def _(j):
        cols = pl.ds(pl.multiple_of(j * dtile, dtile), dtile)
        back = b_recv[:, :, cols].reshape(slots, dtile)
        dx_ref[:, cols] = contract(pick[...], back, 0, 0).astype(BF)

    for i in range(3):
        ring_last(i)

    for done in (meta_done, seq_done, x_done, y_done, o_done, b_done):
        done()

    for i in range(3):

        @pl.loop(0, n_z)
        def _(b):
            twin_copy(i, b).wait_send()

        for s in range(half):
            for way in range(2):
                ring_copy(i, way, s).wait_send()


def on_device(
    n_dp,
    n_ex,
    gen_rows,
    gen_lengths,
    gen_adv,
    destination,
    expert_ids,
    gate_values,
    cotangent,
    w_gate,
    w_up,
    w_down,
):
    rows, width = gen_rows.shape
    seqs = destination.shape[2]
    slot = rows // seqs
    ff = w_gate.shape[2]
    cap = 2 * rows * expert_ids.shape[1] // n_ex
    slots = n_ex * cap
    n_z = n_dp // 2
    per_seq = jnp.stack(
        [destination[0, 0].astype(F32), gen_lengths[0, 0].astype(F32), gen_adv[0, 0].astype(F32)]
    )
    small = jnp.concatenate(
        [
            jnp.repeat(per_seq, slot, axis=1),
            expert_ids.astype(F32).T,
            gate_values.T,
            jnp.zeros((1, rows), F32),
        ]
    )
    vmem = pl.BlockSpec(memory_space=pltpu.VMEM)
    hbm = pl.BlockSpec(memory_space=pl.ANY)
    dma = pltpu.SemaphoreType.DMA
    part, part_d = width // n_dp, ff // n_dp
    buffers = [pltpu.VMEM((n_ex, cap, width), BF)] * 8
    ring = [
        pltpu.VMEM((2, n_z // 2, p, c), BF) for p, c in ((part, ff), (part, ff), (part_d, width))
    ]
    twin = [pltpu.VMEM((n_z, p, c), BF) for p, c in ((part, ff), (part, ff), (part_d, width))]
    outs = pl.pallas_call(
        functools.partial(step_kernel, n_dp, n_ex, slot, cap),
        out_shape=(
            jax.ShapeDtypeStruct((rows, width), BF),
            jax.ShapeDtypeStruct((rows, width), BF),
            jax.ShapeDtypeStruct((part, ff), BF),
            jax.ShapeDtypeStruct((part, ff), BF),
            jax.ShapeDtypeStruct((part_d, width), BF),
        ),
        in_specs=[vmem, vmem, vmem, hbm, hbm, hbm],
        out_specs=[vmem] * 5,
        scratch_shapes=[
            pltpu.VMEM((width, ff), BF),
            pltpu.VMEM((width, ff), BF),
            pltpu.VMEM((ff, width), BF),
            pltpu.VMEM((n_dp, 8, 128), F32),
            pltpu.VMEM((n_dp, 8, 128), F32),
            pltpu.VMEM((n_dp, slot, width), BF),
            pltpu.VMEM((n_dp, slot, width), BF),
            *buffers,
            pltpu.VMEM((slots, rows), BF),
            pltpu.VMEM((slots, rows), BF),
            pltpu.VMEM((slots, rows), BF),
            pltpu.VMEM((slots, ff), F32),
            pltpu.VMEM((slots, ff), F32),
            pltpu.VMEM((slots, ff), BF),
            pltpu.VMEM((slots, ff), BF),
            pltpu.VMEM((slots, ff), BF),
            pltpu.VMEM((width, ff), BF),
            pltpu.VMEM((width, ff), BF),
            pltpu.VMEM((ff, width), BF),
            *twin,
            *ring,
            dma((3,)),
            dma((n_dp,)),
            dma((n_dp,)),
            dma((n_dp,)),
            dma((n_dp,)),
            *([dma((n_ex,))] * 8),
            dma((3, n_z)),
            dma((3, n_z)),
            dma((3, 2, n_z // 2)),
            dma((3, 2, n_z // 2)),
        ],
        compiler_params=pltpu.CompilerParams(
            collective_id=0, has_side_effects=True, vmem_limit_bytes=67043328
        ),
    )(small, gen_rows, cotangent, w_gate[0], w_up[0], w_down[0])
    return outs[0], outs[1], outs[2][None], outs[3][None], outs[4][None]


def solution(mesh):
    n_dp, n_ex = mesh.shape["dp"], mesh.shape["expert"]
    in_specs = (
        P(("dp", "expert"), None),
        P("dp", "expert", None),
        P("dp", "expert", None),
        P("dp", "expert", None),
        P(("dp", "expert"), None),
        P(("dp", "expert"), None),
        P(("dp", "expert"), None),
        P("expert", None, None),
        P("expert", None, None),
        P("expert", None, None),
    )
    out_specs = (
        P(("dp", "expert"), None),
        P(("dp", "expert"), None),
        P("expert", "dp", None),
        P("expert", "dp", None),
        P("expert", "dp", None),
    )
    return jax.shard_map(
        functools.partial(on_device, n_dp, n_ex),
        mesh=mesh,
        in_specs=in_specs,
        out_specs=out_specs,
        check_vma=False,
    )
```

time: 343 us -> 175 us (0.51)
  waiting for transfers between devices: 223 us -> 0 us
  Pallas kernels: 0 us -> 160 us
  matrix products: 61.4 us -> 0 us
  starting transfers between devices: 35.1 us -> 0 us
  between operations: 13.9 us -> 0.65 us
  local copies, waits for them, and re-layouts: 3.86 us -> 8.84 us
    pallas_call x0 -> x1, Pallas kernels: none -> 160 us  [on_device(): pl.pallas_call(functools.partial(step_kernel, n_dp, n_ex, slot, cap), out...]
    all_to_all x6 -> x0, waiting for transfers between devices: 133 us -> none  [the longest x1 29.2 us: on_device(): lax.all_to_all(send_dy, 'expert', split_axis=0, concat_axis=0, tiled=True)]
    reduce_scatter x3 -> x0, waiting for transfers between devices: 89.8 us -> none  [the longest x1 63.3 us: on_device(): lax.psum_scatter(contract(flat_in, up_grad, 0, 0).astype(jnp.bfloat16), '...]
    dot_general x16 -> x0, matrix products: 61.4 us -> none  [the longest x9 37.4 us: contract(): lax.dot_general(left, right, (((left_dim,), (right_dim,)), ((), ())), pre...]
    all_to_all x6 -> x0, starting transfers between devices: 34.8 us -> none  [the longest x1 9.97 us: on_device(): lax.all_to_all(out_meta, 'dp', split_axis=0, concat_axis=0, tiled=True)]
    unnamed x12 -> x5, local copies, waits for them, and re-layouts: 0.94 us -> 8.61 us
  transfers between devices with their start and end apart: 9 -> 0, of which waited for: 8 -> 0; matrix products, arithmetic and copies ran while one was open for 15% -> 0% of each run, Pallas kernels for 0% -> 0%
where the time goes in v1:
time: 175 us; the launch traced here: 173 us
  Pallas kernels  160 us (91%)
  local copies, waits for them, and re-layouts  8.84 us (5%)
  other arithmetic  3.37 us (2%)
    pallas_call x1, Pallas kernels, on_device(): pl.pallas_call(functools.partial(step_kernel, n_dp, n_ex, slot, cap), out...  160 us
    unnamed x5, local copies, waits for them, and re-layouts  8.61 us

profile of v1, /device:TPU:1, one launch (start us, length us, event | category | flops | bytes accessed | tf_op | source)
XLA Modules:
  0.0 172.9 jit_solution(14800759161720976220)
XLA Ops:
  0.6 0.7 bitcast_convert_fusion
  1.3 0.1 pad.3.clone
  1.4 0.7 convert_bitcast_fusion
  2.0 0.7 convert_bitcast_fusion.1
  2.7 0.1 broadcast_in_dim.15
  2.8 0.1 reshape.47
  2.9 1.3 maximum_maximum_fusion.small_ref
  4.2 160.0 %shard_map.137 = (bf16[128,2048]{1,0:T(8,128)(2,1)}, bf16[128,2048]{1,0:T(8,128)(2,1)}, bf16[128,768]{1,0:T(8,128)(2,1)}, bf16[128,768]{1,0:T(8,128)(2,1)}, bf16[48,2048]{1,0:T(8,128)(2,1)}) custom-call(f32[8,128]{1,0:T(8,128)} %maximum_maximum_fusion.small_ref, bf16[128,2048]{1,0:T(8,128)(2,1)} %gen_ref.1, bf16[128,2048]{1,0:T(8,128)(2,1)} %cot_ref.1, ...), custom_call_target="tpu_custom_call" | custom-call | tf_op jit(solution)/shard_map/pallas_call | solution.py:485
  164.2 1.9 %copy.20 = bf16[128,2048]{1,0:T(8,128)(2,1)} copy(bf16[128,2048]{1,0:T(8,128)(2,1)} %get-tuple-element.22) | data formatting | bytes 1048576
  166.1 1.9 %copy.21 = bf16[128,2048]{1,0:T(8,128)(2,1)} copy(bf16[128,2048]{1,0:T(8,128)(2,1)} %get-tuple-element.23) | data formatting | bytes 1048576
  168.0 1.6 copy.22
  169.6 1.6 copy.23
  171.2 1.6 copy.24
  (1 shorter events, 0.0 us)

commit v2 on v1

--- a/solution.py
+++ b/solution.py
@@ -27,9 +27,13 @@
     n_ex,
     slot,
     cap,
-    small_ref,
-    gen_ref,
-    cot_ref,
+    dest_ref,
+    len_ref,
+    adv_ref,
+    ids_ref,
+    gate_ref,
+    gen_hbm,
+    cot_hbm,
     wg_hbm,
     wu_hbm,
     wd_hbm,
@@ -38,11 +42,15 @@
     gg_out,
     gu_out,
     gd_out,
+    gen_ref,
+    cot_ref,
     wg,
     wu,
     wd,
     meta_send,
     meta_recv,
+    scale_send,
+    scale_recv,
     seq_send,
     seq_recv,
     x_send,
@@ -55,7 +63,7 @@
     b_recv,
     pick,
     hi,
-    lo,
+    low,
     fac_a,
     fac_b,
     hid,
@@ -73,6 +81,8 @@
     w_sem,
     meta_ss,
     meta_rs,
+    scale_ss,
+    scale_rs,
     seq_ss,
     seq_rs,
     x_ss,
@@ -98,16 +108,35 @@
     width = gen_ref.shape[1]
     ff = wg.shape[1]
     slots = n_ex * cap
+    lanes = max(cap, 128)
     dtile = min(256, width)
     ftile = min(256, ff)
     nd, nf = width // dtile, ff // ftile
 
-    weights = [
-        pltpu.make_async_copy(src, dst, w_sem.at[i])
-        for i, (src, dst) in enumerate(((wg_hbm, wg), (wu_hbm, wu), (wd_hbm, wd)))
-    ]
-    for copy in weights:
-        copy.start()
+    nx = 1
+    while (nx * 2) * (nx * 2) <= n_ex:
+        nx *= 2
+    ny = n_ex // nx
+    ex, ey = lax.rem(e, nx), lax.div(e, nx)
+
+    def far(d, n):
+        return min(d, n - d)
+
+    tokens = sorted(
+        ((dy, dx) for dy in range(ny) for dx in range(nx)),
+        key=lambda d: -(far(d[0], ny) + far(d[1], nx)),
+    )
+    trainers = sorted(
+        ((dz, dc) for dz in range(n_z) for dc in range(2)), key=lambda d: -(far(d[0], n_z) + d[1])
+    )
+
+    def expert_to(i, sign=1):
+        dy, dx = tokens[i]
+        return lax.rem(ey + sign * dy + ny, ny) * nx + lax.rem(ex + sign * dx + nx, nx)
+
+    def trainer_to(i):
+        dz, dc = trainers[i]
+        return lax.rem(z + dz, n_z) * 2 + lax.rem(core + dc, 2)
 
     barrier = pltpu.get_barrier_semaphore()
 
@@ -121,19 +150,29 @@
             barrier, 1, device_id={"expert": lax.rem(e + o, n_ex)}, device_id_type=MESH
         )
 
+    loads = [
+        pltpu.make_async_copy(src, dst, w_sem.at[i])
+        for i, (src, dst) in enumerate(
+            ((gen_hbm, gen_ref), (cot_hbm, cot_ref), (wg_hbm, wg), (wu_hbm, wu), (wd_hbm, wd))
+        )
+    ]
+    for copy in loads:
+        copy.start()
+
     shift = slot.bit_length() - 1
-    dest_row = small_ref[0:1, :]
-    len_row = small_ref[1:2, :]
-    adv_row = small_ref[2:3, :]
+    seqs = dest_ref.shape[1]
     srow, scol = iota((n_dp * slot, rows), 0), iota((n_dp * slot, rows), 1)
-    spread = (dest_row == (srow >> shift).astype(F32)) & ((srow & (slot - 1)) == (scol & (slot - 1)))
-    spread = spread.astype(BF)
-    mine = dest_row == iota((n_dp, rows), 0).astype(F32)
-    first = (iota((n_dp, rows), 1) & (slot - 1)) == 0
-    len_to = jnp.max(jnp.where(mine, len_row, 0.0), axis=1, keepdims=True)
-    adv_to = jnp.sum(jnp.where(mine & first, adv_row, 0.0), axis=1, keepdims=True)
+    same_place = (srow & (slot - 1)) == (scol & (slot - 1))
+    mine = dest_ref[...] == iota((n_dp, seqs), 0)
+    len_to = jnp.sum(jnp.where(mine, len_ref[...].astype(F32), 0.0), axis=1, keepdims=True)
+    adv_to = jnp.sum(jnp.where(mine, adv_ref[...].astype(F32), 0.0), axis=1, keepdims=True)
     line = iota((n_dp, 8, 128), 1)
     meta_send[...] = jnp.where(line == 0, len_to[:, :, None], adv_to[:, :, None])
+    seq_lanes = ((iota((seqs, rows), 1) >> shift) == iota((seqs, rows), 0)).astype(F32)
+    mine_lanes = jnp.dot(mine.astype(F32), seq_lanes, preferred_element_type=F32)
+    spread = jnp.broadcast_to(mine_lanes[:, None, :], (n_dp, slot, rows)).reshape(n_dp * slot, rows)
+    spread = jnp.where(same_place, spread, 0.0).astype(BF)
+    loads[0].wait()
 
     @pl.loop(0, nd)
     def _(j):
@@ -144,10 +183,12 @@
             .reshape(n_dp, slot, dtile)
         )
 
-    names = iota((n_ex, rows), 0).astype(F32)
-    hit0, hit1 = small_ref[3:4, :] == names, small_ref[4:5, :] == names
+    names = jnp.zeros((n_ex, rows), jnp.int32)
+    for i in range(n_ex):
+        names = jnp.where(iota((n_ex, rows), 0) == i, expert_to(i), names)
+    hit0, hit1 = ids_ref[0:1, :] == names, ids_ref[1:2, :] == names
     routed = hit0 | hit1
-    gate_of = jnp.where(hit0, small_ref[5:6, :], 0.0) + jnp.where(hit1, small_ref[6:7, :], 0.0)
+    gate_of = jnp.where(hit0, gate_ref[0:1, :], 0.0) + jnp.where(hit1, gate_ref[1:2, :], 0.0)
     before = (iota((rows, rows), 0) < iota((rows, rows), 1)).astype(BF)
     pos = jnp.dot(routed.astype(BF), before, preferred_element_type=F32)
     code = jnp.where(routed, pos, -1.0)
@@ -157,55 +198,93 @@
     weighted = jnp.where(hit, gate_of[:, None, :], 0.0).reshape(slots, rows)
     whole = weighted.astype(BF)
     hi[...] = whole
-    lo[...] = (weighted - whole.astype(F32)).astype(BF)
+    low[...] = (weighted - whole.astype(F32)).astype(BF)
+
+    loads[1].wait()
+
+    @pl.loop(0, nd)
+    def _(j):
+        cols = pl.ds(pl.multiple_of(j * dtile, dtile), dtile)
+        y_send[:, :, cols] = (
+            jnp.dot(pick[...], cot_ref[:, cols], preferred_element_type=F32)
+            .astype(BF)
+            .reshape(n_ex, cap, dtile)
+        )
 
     pl.semaphore_wait(barrier, n_dp + n_ex - 2)
 
-    def exchange(axis, me, n, send, recv, ss, rs):
-        def copy(o):
-            peer = lax.rem(me + o, n)
+    def dp_exchange(send, recv, ss, rs):
+        def copy(i):
+            peer = trainer_to(i)
             return pltpu.make_async_remote_copy(
                 src_ref=send.at[peer],
-                dst_ref=recv.at[me],
-                send_sem=ss.at[o],
-                recv_sem=rs.at[o],
-                device_id={axis: peer},
+                dst_ref=recv.at[g],
+                send_sem=ss.at[i],
+                recv_sem=rs.at[i],
+                device_id={"dp": peer},
                 device_id_type=MESH,
             )
 
-        def own():
-            return pltpu.make_async_copy(send.at[me], recv.at[me], ss.at[0])
+        own = pltpu.make_async_copy(send.at[g], recv.at[g], ss.at[n_dp - 1])
 
         def start():
-            own().start()
-
-            @pl.loop(1, n)
-            def _(o):
-                copy(o).start()
+            for i in range(n_dp - 1):
+                copy(i).start()
+            own.start()
 
         def wait_recv():
-            own().wait()
-
-            @pl.loop(1, n)
-            def _(o):
-                copy(o).wait_recv()
+            own.wait()
+            for i in range(n_dp - 1):
+                copy(i).wait_recv()
 
         def wait_send():
-            @pl.loop(1, n)
-            def _(o):
-                copy(o).wait_send()
+            for i in range(n_dp - 1):
+                copy(i).wait_send()
 
         return start, wait_recv, wait_send
 
-    meta_start, meta_wait, meta_done = exchange("dp", g, n_dp, meta_send, meta_recv, meta_ss, meta_rs)
-    seq_start, seq_wait, seq_done = exchange("dp", g, n_dp, seq_send, seq_recv, seq_ss, seq_rs)
-    x_start, x_wait, x_done = exchange("expert", e, n_ex, x_send, x_recv, x_ss, x_rs)
-    y_start, y_wait, y_done = exchange("expert", e, n_ex, y_send, y_recv, y_ss, y_rs)
-    o_start, o_wait, o_done = exchange("expert", e, n_ex, o_send, o_recv, o_ss, o_rs)
-    b_start, b_wait, b_done = exchange("expert", e, n_ex, b_send, b_recv, b_ss, b_rs)
+    def token_exchange(sign, send, recv, ss, rs):
+        def copy(i):
+            return pltpu.make_async_remote_copy(
+                src_ref=send.at[i],
+                dst_ref=recv.at[i],
+                send_sem=ss.at[i],
+                recv_sem=rs.at[i],
+                device_id={"expert": expert_to(i, sign)},
+                device_id_type=MESH,
+            )
+
+        own = pltpu.make_async_copy(send.at[n_ex - 1], recv.at[n_ex - 1], ss.at[n_ex - 1])
+
+        def start(lo=0, hi=n_ex):
+            for i in range(lo, min(hi, n_ex - 1)):
+                copy(i).start()
+            if hi == n_ex:
+                own.start()
+
+        def wait_recv(lo=0, hi=n_ex):
+            if hi == n_ex:
+                own.wait()
+            for i in range(lo, min(hi, n_ex - 1)):
+                copy(i).wait_recv()
+
+        def wait_send():
+            for i in range(n_ex - 1):
+                copy(i).wait_send()
+
+        return start, wait_recv, wait_send
+
+    meta_start, meta_wait, meta_done = dp_exchange(meta_send, meta_recv, meta_ss, meta_rs)
+    seq_start, seq_wait, seq_done = dp_exchange(seq_send, seq_recv, seq_ss, seq_rs)
+    x_start, x_wait, x_done = token_exchange(1, x_send, x_recv, x_ss, x_rs)
+    y_start, y_wait, y_done = token_exchange(1, y_send, y_recv, y_ss, y_rs)
+    v_start, v_wait, v_done = token_exchange(1, scale_send, scale_recv, scale_ss, scale_rs)
+    o_start, o_wait, o_done = token_exchange(-1, o_send, o_recv, o_ss, o_rs)
+    b_start, b_wait, b_done = token_exchange(-1, b_send, b_recv, b_ss, b_rs)
 
     meta_start()
     seq_start()
+    y_start()
     meta_wait()
 
     got_len = meta_recv[:, 0, :]
@@ -219,24 +298,19 @@
     def widen(v):
         return jnp.broadcast_to(v[:, None, :rows], (n_dp, slot, rows)).reshape(n_dp * slot, rows)
 
-    placed = (widen(arrival) == (scol >> shift).astype(F32)) & (
-        (srow & (slot - 1)) == (scol & (slot - 1))
-    )
+    placed = (widen(arrival) == (scol >> shift).astype(F32)) & same_place
     within = (srow & (slot - 1)).astype(F32) < widen(got_len)
     tok_scale = jnp.sum(
         jnp.where(placed & within, widen(per_len), 0.0), axis=0, keepdims=True
     )
     row_scale = jnp.sum(
         jnp.where(hit, (gate_of * tok_scale)[:, None, :], 0.0), axis=2, keepdims=True
-    ).reshape(slots, 1)
-
-    @pl.loop(0, nd)
-    def _(j):
-        cols = pl.ds(pl.multiple_of(j * dtile, dtile), dtile)
-        rowsel = jnp.dot(pick[...], cot_ref[:, cols], preferred_element_type=F32)
-        y_send[:, :, cols] = (rowsel * row_scale).astype(BF).reshape(n_ex, cap, dtile)
-
-    y_start()
+    )
+    on_lane = iota((n_ex, cap, lanes), 1) == iota((n_ex, cap, lanes), 2)
+    scale_send[...] = jnp.broadcast_to(
+        jnp.sum(jnp.where(on_lane, row_scale, 0.0), axis=1, keepdims=True), (n_ex, 8, lanes)
+    )
+    v_start()
     fetch = contract(picked, placed.astype(BF), 1, 1).astype(BF)
     seq_wait()
 
@@ -249,33 +323,52 @@
         )
 
     x_start()
-    for copy in weights:
-        copy.wait()
-    x_wait()
-
-    @pl.loop(0, nf)
-    def _(j):
-        cols = pl.ds(pl.multiple_of(j * ftile, ftile), ftile)
-        x_all = x_recv[...].reshape(slots, width)
-        gate_pre = jnp.dot(x_all, wg[:, cols], preferred_element_type=F32)
-        up_pre = jnp.dot(x_all, wu[:, cols], preferred_element_type=F32)
-        sig = jax.nn.sigmoid(gate_pre)
-        act = gate_pre * sig
-        hid[:, cols] = (act * up_pre).astype(BF)
-        fac_a[:, cols] = up_pre * sig * (1.0 + gate_pre * (1.0 - sig))
-        fac_b[:, cols] = act
+    y_wait()
+    v_wait()
+    scale = jnp.sum(
+        jnp.where(on_lane, scale_recv[:, 0:1, :], 0.0), axis=2, keepdims=True
+    ).reshape(slots, 1)
 
     @pl.loop(0, nd)
     def _(j):
         cols = pl.ds(pl.multiple_of(j * dtile, dtile), dtile)
-        o_send[:, :, cols] = (
-            jnp.dot(hid[...], wd[:, cols], preferred_element_type=F32)
+        y_recv[:, :, cols] = (
+            (y_recv[:, :, cols].reshape(slots, dtile).astype(F32) * scale)
             .astype(BF)
             .reshape(n_ex, cap, dtile)
         )
 
-    o_start()
-    y_wait()
+    for copy in loads[2:]:
+        copy.wait()
+
+    group = n_ex // 2
+    for part in range(2):
+        lo, n_rows = part * group, group * cap
+        here = pl.ds(lo * cap, n_rows)
+        x_wait(lo, lo + group)
+
+        @pl.loop(0, nf)
+        def _(j):
+            cols = pl.ds(pl.multiple_of(j * ftile, ftile), ftile)
+            x_some = x_recv[lo : lo + group].reshape(n_rows, width)
+            gate_pre = jnp.dot(x_some, wg[:, cols], preferred_element_type=F32)
+            up_pre = jnp.dot(x_some, wu[:, cols], preferred_element_type=F32)
+            sig = jax.nn.sigmoid(gate_pre)
+            act = gate_pre * sig
+            hid[here, cols] = (act * up_pre).astype(BF)
+            fac_a[here, cols] = up_pre * sig * (1.0 + gate_pre * (1.0 - sig))
+            fac_b[here, cols] = act
+
+        @pl.loop(0, nd)
+        def _(j):
+            cols = pl.ds(pl.multiple_of(j * dtile, dtile), dtile)
+            o_send[lo : lo + group, :, cols] = (
+                jnp.dot(hid[here, :], wd[:, cols], preferred_element_type=F32)
+                .astype(BF)
+                .reshape(group, cap, dtile)
+            )
+
+        o_start(lo, lo + group)
 
     @pl.loop(0, nf)
     def _(j):
@@ -366,6 +459,36 @@
             + ring[1, half - 1].astype(F32)
         ).astype(BF)
 
+    pair = width // n_z
+
+    def ring_order(k):
+        d = half - lax.div(k + 1, 2)
+        way = 2 * lax.rem(k, 2) - 1
+        return lax.rem(z + way * d + n_z, n_z)
+
+    def gate_up(lo, hi):
+        @pl.loop(lo, hi)
+        def _(k):
+            b = ring_order(k)
+            cols = pl.ds(pl.multiple_of(b * pair, pair), pair)
+            x_part = x_recv[:, :, cols].reshape(slots, pair)
+            grad_g[cols, :] = contract(x_part, gg[...], 0, 0).astype(BF)
+            twin_copy(1, b).start()
+            grad_u[cols, :] = contract(x_part, ug[...], 0, 0).astype(BF)
+            twin_copy(2, b).start()
+
+    def input_rows(lo, hi):
+        @pl.loop(lo, hi)
+        def _(j):
+            cols = pl.ds(pl.multiple_of(j * dtile, dtile), dtile)
+            b_send[:, :, cols] = (
+                (contract(gg[...], wg[cols, :], 1, 1) + contract(ug[...], wu[cols, :], 1, 1))
+                .astype(BF)
+                .reshape(n_ex, cap, dtile)
+            )
+
+    gate_up(0, 1)
+
     @pl.loop(0, nf * nd)
     def _(j):
         units = pl.ds(pl.multiple_of(lax.div(j, nd) * ftile, ftile), ftile)
@@ -376,45 +499,40 @@
 
     @pl.loop(0, n_z)
     def _(k):
-        twin_copy(0, lax.rem(z + half + k, n_z)).start()
-
-    @pl.loop(0, nd)
-    def _(j):
-        cols = pl.ds(pl.multiple_of(j * dtile, dtile), dtile)
-        b_send[:, :, cols] = (
-            (contract(gg[...], wg[cols, :], 1, 1) + contract(ug[...], wu[cols, :], 1, 1))
-            .astype(BF)
-            .reshape(n_ex, cap, dtile)
-        )
-
-    b_start()
-    ring_step(0, 0)
-
-    pair = width // n_z
-
-    @pl.loop(0, n_z)
-    def _(k):
-        b = lax.rem(z + half + k, n_z)
-        cols = pl.ds(pl.multiple_of(b * pair, pair), pair)
-        x_part = x_recv[:, :, cols].reshape(slots, pair)
-        grad_g[cols, :] = contract(x_part, gg[...], 0, 0).astype(BF)
-        grad_u[cols, :] = contract(x_part, ug[...], 0, 0).astype(BF)
-        twin_copy(1, b).start()
-        twin_copy(2, b).start()
+        twin_copy(0, ring_order(k)).start()
 
     ring_step(1, 0)
     ring_step(2, 0)
-    for s in range(1, half):
-        for i in range(3):
-            ring_step(i, s)
-
-    o_wait()
-
-    @pl.loop(0, nd)
-    def _(j):
-        cols = pl.ds(pl.multiple_of(j * dtile, dtile), dtile)
-        back = o_recv[:, :, cols].reshape(slots, dtile)
-        out_ref[:, cols] = (contract(hi[...], back, 0, 0) + contract(lo[...], back, 0, 0)).astype(BF)
+    gate_up(1, 3)
+    ring_step(0, 0)
+    gate_up(3, n_z)
+    ring_step(1, 1)
+    ring_step(2, 1)
+    first = nd * 3 // 8
+    input_rows(0, first)
+    ring_step(0, 1)
+    input_rows(first, nd)
+    b_start()
+
+    def tokens_out():
+        o_wait()
+
+        @pl.loop(0, nd)
+        def _(j):
+            cols = pl.ds(pl.multiple_of(j * dtile, dtile), dtile)
+            back = o_recv[:, :, cols].reshape(slots, dtile)
+            out_ref[:, cols] = (
+                contract(hi[...], back, 0, 0) + contract(low[...], back, 0, 0)
+            ).astype(BF)
+
+    for s in range(2, half):
+        ring_step(1, s)
+        ring_step(2, s)
+        if s == 2:
+            tokens_out()
+        ring_step(0, s)
+    if half < 3:
+        tokens_out()
 
     b_wait()
 
@@ -424,10 +542,10 @@
         back = b_recv[:, :, cols].reshape(slots, dtile)
         dx_ref[:, cols] = contract(pick[...], back, 0, 0).astype(BF)
 
-    for i in range(3):
+    for i in (1, 2, 0):
         ring_last(i)
 
-    for done in (meta_done, seq_done, x_done, y_done, o_done, b_done):
+    for done in (meta_done, v_done, seq_done, x_done, y_done, o_done, b_done):
         done()
 
     for i in range(3):
@@ -439,6 +557,33 @@
         for s in range(half):
             for way in range(2):
                 ring_copy(i, way, s).wait_send()
+
+
+def settle_kernel(*refs):
+    n = (len(refs) - 2) // 3
+    src, dst, held, sems = refs[:n], refs[n : 2 * n], refs[2 * n : 3 * n], refs[3 * n :]
+    ins = [pltpu.make_async_copy(src[i], held[i], sems[0].at[i]) for i in range(n)]
+    outs = [pltpu.make_async_copy(held[i], dst[i], sems[1].at[i]) for i in range(n)]
+    for copy in ins:
+        copy.start()
+    for i in range(n):
+        ins[i].wait()
+        outs[i].start()
+    for copy in outs:
+        copy.wait()
+
+
+def settle(arrays):
+    n = len(arrays)
+    hbm = pl.BlockSpec(memory_space=pl.ANY)
+    return pl.pallas_call(
+        settle_kernel,
+        out_shape=[jax.ShapeDtypeStruct(a.shape, a.dtype) for a in arrays],
+        in_specs=[hbm] * n,
+        out_specs=[hbm] * n,
+        scratch_shapes=[pltpu.VMEM(a.shape, a.dtype) for a in arrays]
+        + [pltpu.SemaphoreType.DMA((n,)), pltpu.SemaphoreType.DMA((n,))],
+    )(*arrays)
 
 
 def on_device(
@@ -462,17 +607,7 @@
     cap = 2 * rows * expert_ids.shape[1] // n_ex
     slots = n_ex * cap
     n_z = n_dp // 2
-    per_seq = jnp.stack(
-        [destination[0, 0].astype(F32), gen_lengths[0, 0].astype(F32), gen_adv[0, 0].astype(F32)]
-    )
-    small = jnp.concatenate(
-        [
-            jnp.repeat(per_seq, slot, axis=1),
-            expert_ids.astype(F32).T,
-            gate_values.T,
-            jnp.zeros((1, rows), F32),
-        ]
-    )
+    lanes = max(cap, 128)
     vmem = pl.BlockSpec(memory_space=pltpu.VMEM)
     hbm = pl.BlockSpec(memory_space=pl.ANY)
     dma = pltpu.SemaphoreType.DMA
@@ -491,14 +626,18 @@
             jax.ShapeDtypeStruct((part, ff), BF),
             jax.ShapeDtypeStruct((part_d, width), BF),
         ),
-        in_specs=[vmem, vmem, vmem, hbm, hbm, hbm],
+        in_specs=[vmem] * 5 + [hbm] * 5,
         out_specs=[vmem] * 5,
         scratch_shapes=[
+            pltpu.VMEM((rows, width), BF),
+            pltpu.VMEM((rows, width), BF),
             pltpu.VMEM((width, ff), BF),
             pltpu.VMEM((width, ff), BF),
             pltpu.VMEM((ff, width), BF),
             pltpu.VMEM((n_dp, 8, 128), F32),
             pltpu.VMEM((n_dp, 8, 128), F32),
+            pltpu.VMEM((n_ex, 8, lanes), F32),
+            pltpu.VMEM((n_ex, 8, lanes), F32),
             pltpu.VMEM((n_dp, slot, width), BF),
             pltpu.VMEM((n_dp, slot, width), BF),
             *buffers,
@@ -515,9 +654,11 @@
             pltpu.VMEM((ff, width), BF),
             *twin,
             *ring,
-            dma((3,)),
+            dma((5,)),
             dma((n_dp,)),
             dma((n_dp,)),
+            dma((n_ex,)),
+            dma((n_ex,)),
             dma((n_dp,)),
             dma((n_dp,)),
             *([dma((n_ex,))] * 8),
@@ -529,7 +670,19 @@
         compiler_params=pltpu.CompilerParams(
             collective_id=0, has_side_effects=True, vmem_limit_bytes=67043328
         ),
-    )(small, gen_rows, cotangent, w_gate[0], w_up[0], w_down[0])
+    )(
+        destination[0],
+        gen_lengths[0],
+        gen_adv[0],
+        expert_ids.T,
+        gate_values.T,
+        gen_rows,
+        cotangent,
+        w_gate[0],
+        w_up[0],
+        w_down[0],
+    )
+    outs = settle(outs)
     return outs[0], outs[1], outs[2][None], outs[3][None], outs[4][None]
 
 

time: 175 us -> 134 us (0.77)
  Pallas kernels: 160 us -> 133 us
  local copies, waits for them, and re-layouts: 8.84 us -> 0 us
  other arithmetic: 3.37 us -> 0 us
    pallas_call x1, Pallas kernels: 160 us -> 131 us  [on_device(): pl.pallas_call(functools.partial(step_kernel, n_dp, n_ex, slot, cap), out...]
    unnamed x5 -> x0, local copies, waits for them, and re-layouts: 8.61 us -> none
    pallas_call x0 -> x1, Pallas kernels: none -> 2.28 us  [settle(): pl.pallas_call(settle_kernel, out_shape=[jax.ShapeDtypeStruct(a.shape, a....]
where the time goes in v2:
time: 134 us
  Pallas kernels  133 us (99%)
    pallas_call x1, Pallas kernels, on_device(): pl.pallas_call(functools.partial(step_kernel, n_dp, n_ex, slot, cap), out...  131 us

profile of v2, /device:TPU:1, one launch (start us, length us, event | category | flops | bytes accessed | tf_op | source)
XLA Modules:
  0.0 133.6 jit_solution(6435923657704764292)
XLA Ops:
  0.6 130.6 %shard_map.137 = (bf16[128,2048]{1,0:T(8,128)(2,1)}, bf16[128,2048]{1,0:T(8,128)(2,1)}, bf16[128,768]{1,0:T(8,128)(2,1)}, bf16[128,768]{1,0:T(8,128)(2,1)}, bf16[48,2048]{1,0:T(8,128)(2,1)}) custom-call(s32[1,8]{1,0:T(1,128)} %bitcast.16, s32[1,8]{1,0:T(1,128)} %bitcast.17, bf16[1,8]{1,0:T(2,128)(2,1)} %bitcast.18, s32[2,128]{1,0:T(2,128)} %bitcast.14, ...), custom_call_target="tpu_custom_call" | custom-call | tf_op jit(solution)/shard_map/pallas_call | solution.py:620
  131.3 2.3 %shard_map.138 = (bf16[128,2048]{1,0:T(8,128)(2,1)}, bf16[128,2048]{1,0:T(8,128)(2,1)}, bf16[128,768]{1,0:T(8,128)(2,1)}, bf16[128,768]{1,0:T(8,128)(2,1)}, bf16[48,2048]{1,0:T(8,128)(2,1)}) custom-call(bf16[128,2048]{1,0:T(8,128)(2,1)} %get-tuple-element.15.refs_0_, bf16[128,2048]{1,0:T(8,128)(2,1)} %get-tuple-element.16.refs_1_, ...), custom_call_target="tpu_custom_call" | custom-call | tf_op jit(solution)/shard_map/pallas_call | solution.py:579

commit v3 on v2

--- a/solution.py
+++ b/solution.py
@@ -37,6 +37,11 @@
     wg_hbm,
     wu_hbm,
     wd_hbm,
+    out_hbm,
+    dx_hbm,
+    gg_hbm,
+    gu_hbm,
+    gd_hbm,
     out_ref,
     dx_ref,
     gg_out,
@@ -64,8 +69,7 @@
     pick,
     hi,
     low,
-    fac_a,
-    fac_b,
+    hidden_grad,
     hid,
     gg,
     ug,
@@ -79,20 +83,14 @@
     ring_u,
     ring_d,
     w_sem,
-    meta_ss,
-    meta_rs,
-    scale_ss,
-    scale_rs,
-    seq_ss,
-    seq_rs,
-    x_ss,
-    x_rs,
-    y_ss,
-    y_rs,
-    o_ss,
-    o_rs,
-    b_ss,
-    b_rs,
+    store_sem,
+    meta_sem,
+    scale_sem,
+    seq_sem,
+    x_sem,
+    y_sem,
+    o_sem,
+    b_sem,
     twin_ss,
     twin_rs,
     ring_ss,
@@ -108,6 +106,7 @@
     width = gen_ref.shape[1]
     ff = wg.shape[1]
     slots = n_ex * cap
+    hc = cap // 2
     lanes = max(cap, 128)
     dtile = min(256, width)
     ftile = min(256, ff)
@@ -183,6 +182,76 @@
             .reshape(n_dp, slot, dtile)
         )
 
+    def dp_exchange(send, recv, sems):
+        def copy(src, dst, peer):
+            return pltpu.make_async_remote_copy(
+                src_ref=src,
+                dst_ref=dst,
+                send_sem=sems.at[0],
+                recv_sem=sems.at[1],
+                device_id={"dp": peer},
+                device_id_type=MESH,
+            )
+
+        own = pltpu.make_async_copy(send.at[g], recv.at[g], sems.at[2])
+        others = pl.ds(0, n_dp - 1)
+        every = copy(send.at[others], recv.at[others], trainer_to(0))
+
+        def start():
+            for i in range(n_dp - 1):
+                peer = trainer_to(i)
+                copy(send.at[peer], recv.at[g], peer).start()
+            own.start()
+
+        def wait_recv():
+            own.wait()
+            every.wait_recv()
+
+        return start, wait_recv, every.wait_send
+
+    def token_exchange(sign, send, recv, sems):
+        def copy(p, i):
+            return pltpu.make_async_remote_copy(
+                src_ref=send.at[p, i],
+                dst_ref=recv.at[p, i],
+                send_sem=sems.at[p, 0],
+                recv_sem=sems.at[p, 1],
+                device_id={"expert": expert_to(0 if isinstance(i, pl.Slice) else i, sign)},
+                device_id_type=MESH,
+            )
+
+        last = n_ex - 1
+
+        def own(p):
+            return pltpu.make_async_copy(send.at[p, last], recv.at[p, last], sems.at[p, 2])
+
+        def start(p):
+            for i in range(last):
+                copy(p, i).start()
+            own(p).start()
+
+        def wait_recv(p):
+            own(p).wait()
+            copy(p, pl.ds(0, last)).wait_recv()
+
+        def wait_send():
+            for p in range(send.shape[0]):
+                copy(p, pl.ds(0, last)).wait_send()
+
+        return start, wait_recv, wait_send
+
+    meta_start, meta_wait, meta_done = dp_exchange(meta_send, meta_recv, meta_sem)
+    seq_start, seq_wait, seq_done = dp_exchange(seq_send, seq_recv, seq_sem)
+    x_start, x_wait, x_done = token_exchange(1, x_send, x_recv, x_sem)
+    y_start, y_wait, y_done = token_exchange(1, y_send, y_recv, y_sem)
+    v_start, v_wait, v_done = token_exchange(1, scale_send, scale_recv, scale_sem)
+    o_start, o_wait, o_done = token_exchange(-1, o_send, o_recv, o_sem)
+    b_start, b_wait, b_done = token_exchange(-1, b_send, b_recv, b_sem)
+
+    pl.semaphore_wait(barrier, n_dp + n_ex - 2)
+    meta_start()
+    seq_start()
+
     names = jnp.zeros((n_ex, rows), jnp.int32)
     for i in range(n_ex):
         names = jnp.where(iota((n_ex, rows), 0) == i, expert_to(i), names)
@@ -192,10 +261,11 @@
     before = (iota((rows, rows), 0) < iota((rows, rows), 1)).astype(BF)
     pos = jnp.dot(routed.astype(BF), before, preferred_element_type=F32)
     code = jnp.where(routed, pos, -1.0)
-    hit = code[:, None, :] == iota((n_ex, cap, rows), 1).astype(F32)
+    place = iota((2, n_ex, hc, rows), 0) * hc + iota((2, n_ex, hc, rows), 2)
+    hit = code[None, :, None, :] == place.astype(F32)
     picked = hit.astype(BF).reshape(slots, rows)
     pick[...] = picked
-    weighted = jnp.where(hit, gate_of[:, None, :], 0.0).reshape(slots, rows)
+    weighted = jnp.where(hit, gate_of[None, :, None, :], 0.0).reshape(slots, rows)
     whole = weighted.astype(BF)
     hi[...] = whole
     low[...] = (weighted - whole.astype(F32)).astype(BF)
@@ -205,86 +275,14 @@
     @pl.loop(0, nd)
     def _(j):
         cols = pl.ds(pl.multiple_of(j * dtile, dtile), dtile)
-        y_send[:, :, cols] = (
+        y_send[:, :, :, cols] = (
             jnp.dot(pick[...], cot_ref[:, cols], preferred_element_type=F32)
             .astype(BF)
-            .reshape(n_ex, cap, dtile)
-        )
-
-    pl.semaphore_wait(barrier, n_dp + n_ex - 2)
-
-    def dp_exchange(send, recv, ss, rs):
-        def copy(i):
-            peer = trainer_to(i)
-            return pltpu.make_async_remote_copy(
-                src_ref=send.at[peer],
-                dst_ref=recv.at[g],
-                send_sem=ss.at[i],
-                recv_sem=rs.at[i],
-                device_id={"dp": peer},
-                device_id_type=MESH,
-            )
-
-        own = pltpu.make_async_copy(send.at[g], recv.at[g], ss.at[n_dp - 1])
-
-        def start():
-            for i in range(n_dp - 1):
-                copy(i).start()
-            own.start()
-
-        def wait_recv():
-            own.wait()
-            for i in range(n_dp - 1):
-                copy(i).wait_recv()
-
-        def wait_send():
-            for i in range(n_dp - 1):
-                copy(i).wait_send()
-
-        return start, wait_recv, wait_send
-
-    def token_exchange(sign, send, recv, ss, rs):
-        def copy(i):
-            return pltpu.make_async_remote_copy(
-                src_ref=send.at[i],
-                dst_ref=recv.at[i],
-                send_sem=ss.at[i],
-                recv_sem=rs.at[i],
-                device_id={"expert": expert_to(i, sign)},
-                device_id_type=MESH,
-            )
-
-        own = pltpu.make_async_copy(send.at[n_ex - 1], recv.at[n_ex - 1], ss.at[n_ex - 1])
-
-        def start(lo=0, hi=n_ex):
-            for i in range(lo, min(hi, n_ex - 1)):
-                copy(i).start()
-            if hi == n_ex:
-                own.start()
-
-        def wait_recv(lo=0, hi=n_ex):
-            if hi == n_ex:
-                own.wait()
-            for i in range(lo, min(hi, n_ex - 1)):
-                copy(i).wait_recv()
-
-        def wait_send():
-            for i in range(n_ex - 1):
-                copy(i).wait_send()
-
-        return start, wait_recv, wait_send
-
-    meta_start, meta_wait, meta_done = dp_exchange(meta_send, meta_recv, meta_ss, meta_rs)
-    seq_start, seq_wait, seq_done = dp_exchange(seq_send, seq_recv, seq_ss, seq_rs)
-    x_start, x_wait, x_done = token_exchange(1, x_send, x_recv, x_ss, x_rs)
-    y_start, y_wait, y_done = token_exchange(1, y_send, y_recv, y_ss, y_rs)
-    v_start, v_wait, v_done = token_exchange(1, scale_send, scale_recv, scale_ss, scale_rs)
-    o_start, o_wait, o_done = token_exchange(-1, o_send, o_recv, o_ss, o_rs)
-    b_start, b_wait, b_done = token_exchange(-1, b_send, b_recv, b_ss, b_rs)
-
-    meta_start()
-    seq_start()
-    y_start()
+            .reshape(2, n_ex, hc, dtile)
+        )
+
+    y_start(0)
+    y_start(1)
     meta_wait()
 
     got_len = meta_recv[:, 0, :]
@@ -304,13 +302,14 @@
         jnp.where(placed & within, widen(per_len), 0.0), axis=0, keepdims=True
     )
     row_scale = jnp.sum(
-        jnp.where(hit, (gate_of * tok_scale)[:, None, :], 0.0), axis=2, keepdims=True
-    )
-    on_lane = iota((n_ex, cap, lanes), 1) == iota((n_ex, cap, lanes), 2)
-    scale_send[...] = jnp.broadcast_to(
-        jnp.sum(jnp.where(on_lane, row_scale, 0.0), axis=1, keepdims=True), (n_ex, 8, lanes)
-    )
-    v_start()
+        jnp.where(hit, (gate_of * tok_scale)[None, :, None, :], 0.0), axis=3, keepdims=True
+    )
+    lane_of = iota((2, n_ex, hc, lanes), 0) * hc + iota((2, n_ex, hc, lanes), 2)
+    on_lane = lane_of == iota((2, n_ex, hc, lanes), 3)
+    spread_scale = jnp.where(on_lane, row_scale, 0.0)
+    spread_scale = jnp.sum(spread_scale[0] + spread_scale[1], axis=1, keepdims=True)
+    scale_send[0] = jnp.broadcast_to(spread_scale, (n_ex, 8, lanes))
+    v_start(0)
     fetch = contract(picked, placed.astype(BF), 1, 1).astype(BF)
     seq_wait()
 
@@ -318,65 +317,77 @@
     def _(j):
         cols = pl.ds(pl.multiple_of(j * dtile, dtile), dtile)
         source = seq_recv[:, :, cols].reshape(n_dp * slot, dtile)
-        x_send[:, :, cols] = (
-            jnp.dot(fetch, source, preferred_element_type=F32).astype(BF).reshape(n_ex, cap, dtile)
-        )
-
-    x_start()
-    y_wait()
-    v_wait()
+        x_send[:, :, :, cols] = (
+            jnp.dot(fetch, source, preferred_element_type=F32)
+            .astype(BF)
+            .reshape(2, n_ex, hc, dtile)
+        )
+
+    x_start(0)
+    x_start(1)
+    y_wait(0)
+    y_wait(1)
+    v_wait(0)
     scale = jnp.sum(
-        jnp.where(on_lane, scale_recv[:, 0:1, :], 0.0), axis=2, keepdims=True
+        jnp.where(on_lane, scale_recv[:, :, 0:1, :], 0.0), axis=3, keepdims=True
     ).reshape(slots, 1)
 
     @pl.loop(0, nd)
     def _(j):
         cols = pl.ds(pl.multiple_of(j * dtile, dtile), dtile)
-        y_recv[:, :, cols] = (
-            (y_recv[:, :, cols].reshape(slots, dtile).astype(F32) * scale)
+        y_recv[:, :, :, cols] = (
+            (y_recv[:, :, :, cols].reshape(slots, dtile).astype(F32) * scale)
             .astype(BF)
-            .reshape(n_ex, cap, dtile)
+            .reshape(2, n_ex, hc, dtile)
         )
 
     for copy in loads[2:]:
         copy.wait()
 
-    group = n_ex // 2
-    for part in range(2):
-        lo, n_rows = part * group, group * cap
-        here = pl.ds(lo * cap, n_rows)
-        x_wait(lo, lo + group)
+    @pl.loop(0, nf)
+    def _(j):
+        cols = pl.ds(pl.multiple_of(j * ftile, ftile), ftile)
+        hidden_grad[:, cols] = contract(y_recv[...].reshape(slots, width), wd[cols, :], 1, 1)
+
+    n_rows = n_ex * hc
+
+    def hidden_units(p):
+        here = pl.ds(p * n_rows, n_rows)
 
         @pl.loop(0, nf)
         def _(j):
             cols = pl.ds(pl.multiple_of(j * ftile, ftile), ftile)
-            x_some = x_recv[lo : lo + group].reshape(n_rows, width)
+            x_some = x_recv[p].reshape(n_rows, width)
             gate_pre = jnp.dot(x_some, wg[:, cols], preferred_element_type=F32)
             up_pre = jnp.dot(x_some, wu[:, cols], preferred_element_type=F32)
             sig = jax.nn.sigmoid(gate_pre)
             act = gate_pre * sig
             hid[here, cols] = (act * up_pre).astype(BF)
-            fac_a[here, cols] = up_pre * sig * (1.0 + gate_pre * (1.0 - sig))
-            fac_b[here, cols] = act
+            down = hidden_grad[here, cols]
+            gg[here, cols] = (down * up_pre * sig * (1.0 + gate_pre * (1.0 - sig))).astype(BF)
+            ug[here, cols] = (down * act).astype(BF)
+
+    def output_rows(p):
+        here = pl.ds(p * n_rows, n_rows)
 
         @pl.loop(0, nd)
         def _(j):
             cols = pl.ds(pl.multiple_of(j * dtile, dtile), dtile)
-            o_send[lo : lo + group, :, cols] = (
+            o_send[p, :, :, cols] = (
                 jnp.dot(hid[here, :], wd[:, cols], preferred_element_type=F32)
                 .astype(BF)
-                .reshape(group, cap, dtile)
+                .reshape(n_ex, hc, dtile)
             )
 
-        o_start(lo, lo + group)
-
-    @pl.loop(0, nf)
-    def _(j):
-        cols = pl.ds(pl.multiple_of(j * ftile, ftile), ftile)
-        y_all = y_recv[...].reshape(slots, width)
-        hidden_grad = contract(y_all, wd[cols, :], 1, 1)
-        gg[:, cols] = (hidden_grad * fac_a[:, cols]).astype(BF)
-        ug[:, cols] = (hidden_grad * fac_b[:, cols]).astype(BF)
+    def input_rows():
+        @pl.loop(0, nd)
+        def _(j):
+            cols = pl.ds(pl.multiple_of(j * dtile, dtile), dtile)
+            b_send[:, :, :, cols] = (
+                (contract(gg[...], wg[cols, :], 1, 1) + contract(ug[...], wu[cols, :], 1, 1))
+                .astype(BF)
+                .reshape(2, n_ex, hc, dtile)
+            )
 
     grads = ((grad_d, twin_d, ring_d, gd_out), (grad_g, twin_g, ring_g, gg_out), (grad_u, twin_u, ring_u, gu_out))
 
@@ -388,7 +399,7 @@
         return pltpu.make_async_remote_copy(
             src_ref=grads[i][0].at[block(i, b, 1 - core)],
             dst_ref=grads[i][1].at[b],
-            send_sem=twin_ss.at[i, b],
+            send_sem=twin_ss.at[i],
             recv_sem=twin_rs.at[i, b],
             device_id={"dp": g + 1 - 2 * core},
             device_id_type=MESH,
@@ -406,7 +417,7 @@
         return pltpu.make_async_remote_copy(
             src_ref=grad.at[block(i, b, core), cols],
             dst_ref=ring.at[way, s, :, cols],
-            send_sem=ring_ss.at[i, way, s],
+            send_sem=ring_ss.at[i],
             recv_sem=ring_rs.at[i, way, s],
             device_id={"dp": lax.rem(g + 2 * (1 - 2 * way) + n_dp, n_dp)},
             device_id_type=MESH,
@@ -471,92 +482,130 @@
         def _(k):
             b = ring_order(k)
             cols = pl.ds(pl.multiple_of(b * pair, pair), pair)
-            x_part = x_recv[:, :, cols].reshape(slots, pair)
+            x_part = x_recv[:, :, :, cols].reshape(slots, pair)
             grad_g[cols, :] = contract(x_part, gg[...], 0, 0).astype(BF)
             twin_copy(1, b).start()
             grad_u[cols, :] = contract(x_part, ug[...], 0, 0).astype(BF)
             twin_copy(2, b).start()
 
-    def input_rows(lo, hi):
-        @pl.loop(lo, hi)
+    def down_units(lo, hi):
+        @pl.loop(lo * nd, hi * nd)
+        def _(j):
+            units = pl.ds(pl.multiple_of(lax.div(j, nd) * ftile, ftile), ftile)
+            cols = pl.ds(pl.multiple_of(lax.rem(j, nd) * dtile, dtile), dtile)
+            grad_d[units, cols] = contract(
+                hid[:, units], y_recv[:, :, :, cols].reshape(slots, dtile), 0, 0
+            ).astype(BF)
+
+    def tokens_out():
+        o_wait(0)
+        o_wait(1)
+
+        @pl.loop(0, nd)
         def _(j):
             cols = pl.ds(pl.multiple_of(j * dtile, dtile), dtile)
-            b_send[:, :, cols] = (
-                (contract(gg[...], wg[cols, :], 1, 1) + contract(ug[...], wu[cols, :], 1, 1))
-                .astype(BF)
-                .reshape(n_ex, cap, dtile)
+            back = o_recv[:, :, :, cols].reshape(slots, dtile)
+            out_ref[:, cols] = (
+                contract(hi[...], back, 0, 0) + contract(low[...], back, 0, 0)
+            ).astype(BF)
+
+        stores[0].start()
+
+    def tokens_dx():
+        b_wait(0)
+        b_wait(1)
+
+        @pl.loop(0, nd)
+        def _(j):
+            cols = pl.ds(pl.multiple_of(j * dtile, dtile), dtile)
+            back = b_recv[:, :, :, cols].reshape(slots, dtile)
+            dx_ref[:, cols] = contract(pick[...], back, 0, 0).astype(BF)
+
+        stores[1].start()
+
+    stores = [
+        pltpu.make_async_copy(src, dst, store_sem.at[i])
+        for i, (src, dst) in enumerate(
+            (
+                (out_ref, out_hbm),
+                (dx_ref, dx_hbm),
+                (gg_out, gg_hbm),
+                (gu_out, gu_hbm),
+                (gd_out, gd_hbm),
             )
-
+        )
+    ]
+    cut1, cut2 = nf // 3, nf * 2 // 3
+
+    x_wait(0)
+    hidden_units(0)
+    output_rows(0)
+    x_wait(1)
+    o_start(0)
+    hidden_units(1)
     gate_up(0, 1)
-
-    @pl.loop(0, nf * nd)
-    def _(j):
-        units = pl.ds(pl.multiple_of(lax.div(j, nd) * ftile, ftile), ftile)
-        cols = pl.ds(pl.multiple_of(lax.rem(j, nd) * dtile, dtile), dtile)
-        grad_d[units, cols] = contract(
-            hid[:, units], y_recv[:, :, cols].reshape(slots, dtile), 0, 0
-        ).astype(BF)
+    gate_up(1, 3)
+    ring_step(1, 0)
+    ring_step(2, 0)
+    output_rows(1)
+    o_start(1)
+    down_units(0, cut1)
+    ring_step(1, 1)
+    down_units(cut1, cut2)
+    ring_step(2, 1)
+    down_units(cut2, nf)
 
     @pl.loop(0, n_z)
     def _(k):
         twin_copy(0, ring_order(k)).start()
 
-    ring_step(1, 0)
-    ring_step(2, 0)
-    gate_up(1, 3)
+    gate_up(3, min(5, n_z))
     ring_step(0, 0)
-    gate_up(3, n_z)
-    ring_step(1, 1)
-    ring_step(2, 1)
-    first = nd * 3 // 8
-    input_rows(0, first)
+    if half > 2:
+        ring_step(1, 2)
+    input_rows()
+    b_start(0)
+    b_start(1)
+    if n_z > 5:
+        gate_up(5, n_z)
+    if half > 2:
+        ring_step(2, 2)
     ring_step(0, 1)
-    input_rows(first, nd)
-    b_start()
-
-    def tokens_out():
-        o_wait()
-
-        @pl.loop(0, nd)
-        def _(j):
-            cols = pl.ds(pl.multiple_of(j * dtile, dtile), dtile)
-            back = o_recv[:, :, cols].reshape(slots, dtile)
-            out_ref[:, cols] = (
-                contract(hi[...], back, 0, 0) + contract(low[...], back, 0, 0)
-            ).astype(BF)
-
-    for s in range(2, half):
-        ring_step(1, s)
-        ring_step(2, s)
-        if s == 2:
-            tokens_out()
-        ring_step(0, s)
-    if half < 3:
-        tokens_out()
-
-    b_wait()
-
-    @pl.loop(0, nd)
-    def _(j):
-        cols = pl.ds(pl.multiple_of(j * dtile, dtile), dtile)
-        back = b_recv[:, :, cols].reshape(slots, dtile)
-        dx_ref[:, cols] = contract(pick[...], back, 0, 0).astype(BF)
-
+    if half > 3:
+        ring_step(1, 3)
+    tokens_out()
+    if half > 2:
+        ring_step(0, 2)
+    if half > 3:
+        ring_step(2, 3)
+        ring_step(0, 3)
+    for s in range(4, half):
+        for i in (1, 2, 0):
+            ring_step(i, s)
+    tokens_dx()
     for i in (1, 2, 0):
         ring_last(i)
+        stores[(4, 2, 3)[i]].start()
+
+    for copy in stores:
+        copy.wait()
 
     for done in (meta_done, v_done, seq_done, x_done, y_done, o_done, b_done):
         done()
 
     for i in range(3):
-
-        @pl.loop(0, n_z)
-        def _(b):
-            twin_copy(i, b).wait_send()
-
-        for s in range(half):
-            for way in range(2):
-                ring_copy(i, way, s).wait_send()
+        grad, twin, _, _ = grads[i]
+        part = twin.shape[1]
+        for sem, count in ((twin_ss, n_z), (ring_ss, n_z - 1)):
+            rows_sent = pl.ds(0, count * part)
+            pltpu.make_async_remote_copy(
+                src_ref=grad.at[rows_sent],
+                dst_ref=grad.at[rows_sent],
+                send_sem=sem.at[i],
+                recv_sem=sem.at[i],
+                device_id={"dp": g + 1 - 2 * core},
+                device_id_type=MESH,
+            ).wait_send()
 
 
 def settle_kernel(*refs):
@@ -612,7 +661,7 @@
     hbm = pl.BlockSpec(memory_space=pl.ANY)
     dma = pltpu.SemaphoreType.DMA
     part, part_d = width // n_dp, ff // n_dp
-    buffers = [pltpu.VMEM((n_ex, cap, width), BF)] * 8
+    buffers = [pltpu.VMEM((2, n_ex, cap // 2, width), BF)] * 8
     ring = [
         pltpu.VMEM((2, n_z // 2, p, c), BF) for p, c in ((part, ff), (part, ff), (part_d, width))
     ]
@@ -627,8 +676,13 @@
             jax.ShapeDtypeStruct((part_d, width), BF),
         ),
         in_specs=[vmem] * 5 + [hbm] * 5,
-        out_specs=[vmem] * 5,
+        out_specs=[hbm] * 5,
         scratch_shapes=[
+            pltpu.VMEM((rows, width), BF),
+            pltpu.VMEM((rows, width), BF),
+            pltpu.VMEM((part, ff), BF),
+            pltpu.VMEM((part, ff), BF),
+            pltpu.VMEM((part_d, width), BF),
             pltpu.VMEM((rows, width), BF),
             pltpu.VMEM((rows, width), BF),
             pltpu.VMEM((width, ff), BF),
@@ -636,15 +690,14 @@
             pltpu.VMEM((ff, width), BF),
             pltpu.VMEM((n_dp, 8, 128), F32),
             pltpu.VMEM((n_dp, 8, 128), F32),
-            pltpu.VMEM((n_ex, 8, lanes), F32),
-            pltpu.VMEM((n_ex, 8, lanes), F32),
+            pltpu.VMEM((1, n_ex, 8, lanes), F32),
+            pltpu.VMEM((1, n_ex, 8, lanes), F32),
             pltpu.VMEM((n_dp, slot, width), BF),
             pltpu.VMEM((n_dp, slot, width), BF),
             *buffers,
             pltpu.VMEM((slots, rows), BF),
             pltpu.VMEM((slots, rows), BF),
             pltpu.VMEM((slots, rows), BF),
-            pltpu.VMEM((slots, ff), F32),
             pltpu.VMEM((slots, ff), F32),
             pltpu.VMEM((slots, ff), BF),
             pltpu.VMEM((slots, ff), BF),
@@ -655,16 +708,14 @@
             *twin,
             *ring,
             dma((5,)),
-            dma((n_dp,)),
-            dma((n_dp,)),
-            dma((n_ex,)),
-            dma((n_ex,)),
-            dma((n_dp,)),
-            dma((n_dp,)),
-            *([dma((n_ex,))] * 8),
+            dma((5,)),
+            dma((3,)),
+            dma((1, 3)),
+            dma((3,)),
+            *([dma((2, 3))] * 4),
+            dma((3,)),
             dma((3, n_z)),
-            dma((3, n_z)),
-            dma((3, 2, n_z // 2)),
+            dma((3,)),
             dma((3, 2, n_z // 2)),
         ],
         compiler_params=pltpu.CompilerParams(

time: 134 us -> 125 us (0.933); the launches traced: 134 us -> 123 us
  Pallas kernels: 133 us -> 122 us
    pallas_call x1, Pallas kernels: 131 us -> 120 us  [on_device(): pl.pallas_call(functools.partial(step_kernel, n_dp, n_ex, slot, cap), out...]
where the time goes in v3:
time: 125 us; the launch traced here: 123 us
  Pallas kernels  122 us (98%)
    pallas_call x1, Pallas kernels, on_device(): pl.pallas_call(functools.partial(step_kernel, n_dp, n_ex, slot, cap), out...  120 us

profile of v3, /device:TPU:1, one launch (start us, length us, event | category | flops | bytes accessed | tf_op | source)
XLA Modules:
  0.0 122.8 jit_solution(7639940410304885056)
XLA Ops:
  0.6 119.8 %shard_map.137 = (bf16[128,2048]{1,0:T(8,128)(2,1)}, bf16[128,2048]{1,0:T(8,128)(2,1)}, bf16[128,768]{1,0:T(8,128)(2,1)}, bf16[128,768]{1,0:T(8,128)(2,1)}, bf16[48,2048]{1,0:T(8,128)(2,1)}) custom-call(s32[1,8]{1,0:T(1,128)} %bitcast.16, s32[1,8]{1,0:T(1,128)} %bitcast.17, bf16[1,8]{1,0:T(2,128)(2,1)} %bitcast.18, s32[2,128]{1,0:T(2,128)} %bitcast.14, ...), custom_call_target="tpu_custom_call" | custom-call | tf_op jit(solution)/shard_map/pallas_call | solution.py:669
  120.5 2.3 %shard_map.138 = (bf16[128,2048]{1,0:T(8,128)(2,1)}, bf16[128,2048]{1,0:T(8,128)(2,1)}, bf16[128,768]{1,0:T(8,128)(2,1)}, bf16[128,768]{1,0:T(8,128)(2,1)}, bf16[48,2048]{1,0:T(8,128)(2,1)}) custom-call(bf16[128,2048]{1,0:T(8,128)(2,1)} %get-tuple-element.15.refs_0_, bf16[128,2048]{1,0:T(8,128)(2,1)} %get-tuple-element.16.refs_1_, ...), custom_call_target="tpu_custom_call" | custom-call | tf_op jit(solution)/shard_map/pallas_call | solution.py:628

commit v4 on v3

--- a/solution.py
+++ b/solution.py
@@ -10,6 +10,7 @@
 MESH = pl.DeviceIdType.MESH
 BF = jnp.bfloat16
 F32 = jnp.float32
+WIDE = 1024
 
 
 def contract(left, right, left_dim, right_dim):
@@ -37,11 +38,6 @@
     wg_hbm,
     wu_hbm,
     wd_hbm,
-    out_hbm,
-    dx_hbm,
-    gg_hbm,
-    gu_hbm,
-    gd_hbm,
     out_ref,
     dx_ref,
     gg_out,
@@ -69,10 +65,10 @@
     pick,
     hi,
     low,
+    dx_half,
     hidden_grad,
     hid,
-    gg,
-    ug,
+    both,
     grad_g,
     grad_u,
     grad_d,
@@ -83,7 +79,6 @@
     ring_u,
     ring_d,
     w_sem,
-    store_sem,
     meta_sem,
     scale_sem,
     seq_sem,
@@ -272,17 +267,21 @@
 
     loads[1].wait()
 
-    @pl.loop(0, nd)
-    def _(j):
-        cols = pl.ds(pl.multiple_of(j * dtile, dtile), dtile)
-        y_send[:, :, :, cols] = (
-            jnp.dot(pick[...], cot_ref[:, cols], preferred_element_type=F32)
-            .astype(BF)
-            .reshape(2, n_ex, hc, dtile)
-        )
-
-    y_start(0)
-    y_start(1)
+    n_rows = n_ex * hc
+
+    for p in range(2):
+
+        @pl.loop(0, nd)
+        def _(j):
+            cols = pl.ds(pl.multiple_of(j * dtile, dtile), dtile)
+            y_send[p, :, :, cols] = (
+                jnp.dot(pick[p * n_rows : (p + 1) * n_rows, :], cot_ref[:, cols], preferred_element_type=F32)
+                .astype(BF)
+                .reshape(n_ex, hc, dtile)
+            )
+
+        y_start(p)
+
     meta_wait()
 
     got_len = meta_recv[:, 0, :]
@@ -313,18 +312,20 @@
     fetch = contract(picked, placed.astype(BF), 1, 1).astype(BF)
     seq_wait()
 
-    @pl.loop(0, nd)
-    def _(j):
-        cols = pl.ds(pl.multiple_of(j * dtile, dtile), dtile)
-        source = seq_recv[:, :, cols].reshape(n_dp * slot, dtile)
-        x_send[:, :, :, cols] = (
-            jnp.dot(fetch, source, preferred_element_type=F32)
-            .astype(BF)
-            .reshape(2, n_ex, hc, dtile)
-        )
-
-    x_start(0)
-    x_start(1)
+    for p in range(2):
+
+        @pl.loop(0, nd)
+        def _(j):
+            cols = pl.ds(pl.multiple_of(j * dtile, dtile), dtile)
+            source = seq_recv[:, :, cols].reshape(n_dp * slot, dtile)
+            x_send[p, :, :, cols] = (
+                jnp.dot(fetch[p * n_rows : (p + 1) * n_rows, :], source, preferred_element_type=F32)
+                .astype(BF)
+                .reshape(n_ex, hc, dtile)
+            )
+
+        x_start(p)
+
     y_wait(0)
     y_wait(1)
     v_wait(0)
@@ -348,8 +349,6 @@
     def _(j):
         cols = pl.ds(pl.multiple_of(j * ftile, ftile), ftile)
         hidden_grad[:, cols] = contract(y_recv[...].reshape(slots, width), wd[cols, :], 1, 1)
-
-    n_rows = n_ex * hc
 
     def hidden_units(p):
         here = pl.ds(p * n_rows, n_rows)
@@ -364,8 +363,11 @@
             act = gate_pre * sig
             hid[here, cols] = (act * up_pre).astype(BF)
             down = hidden_grad[here, cols]
-            gg[here, cols] = (down * up_pre * sig * (1.0 + gate_pre * (1.0 - sig))).astype(BF)
-            ug[here, cols] = (down * act).astype(BF)
+            both[here, cols] = (
+                down * up_pre * sig * (1.0 + gate_pre * (1.0 - sig))
+            ).astype(BF)
+            ups = pl.ds(pl.multiple_of(ff + j * ftile, ftile), ftile)
+            both[here, ups] = (down * act).astype(BF)
 
     def output_rows(p):
         here = pl.ds(p * n_rows, n_rows)
@@ -379,12 +381,15 @@
                 .reshape(n_ex, hc, dtile)
             )
 
-    def input_rows():
-        @pl.loop(0, nd)
+    def input_rows(lo, hi):
+        @pl.loop(lo, hi)
         def _(j):
             cols = pl.ds(pl.multiple_of(j * dtile, dtile), dtile)
             b_send[:, :, :, cols] = (
-                (contract(gg[...], wg[cols, :], 1, 1) + contract(ug[...], wu[cols, :], 1, 1))
+                (
+                    contract(both[:, :ff], wg[cols, :], 1, 1)
+                    + contract(both[:, ff:], wu[cols, :], 1, 1)
+                )
                 .astype(BF)
                 .reshape(2, n_ex, hc, dtile)
             )
@@ -483,18 +488,23 @@
             b = ring_order(k)
             cols = pl.ds(pl.multiple_of(b * pair, pair), pair)
             x_part = x_recv[:, :, :, cols].reshape(slots, pair)
-            grad_g[cols, :] = contract(x_part, gg[...], 0, 0).astype(BF)
+            sums = contract(x_part, both[...], 0, 0).astype(BF)
+            grad_g[cols, :] = sums[:, :ff]
+            grad_u[cols, :] = sums[:, ff:]
             twin_copy(1, b).start()
-            grad_u[cols, :] = contract(x_part, ug[...], 0, 0).astype(BF)
             twin_copy(2, b).start()
 
+    wide = min(WIDE, width)
+
     def down_units(lo, hi):
-        @pl.loop(lo * nd, hi * nd)
+        per = width // wide
+
+        @pl.loop(lo * per, hi * per)
         def _(j):
-            units = pl.ds(pl.multiple_of(lax.div(j, nd) * ftile, ftile), ftile)
-            cols = pl.ds(pl.multiple_of(lax.rem(j, nd) * dtile, dtile), dtile)
+            units = pl.ds(pl.multiple_of(lax.div(j, per) * ftile, ftile), ftile)
+            cols = pl.ds(pl.multiple_of(lax.rem(j, per) * wide, wide), wide)
             grad_d[units, cols] = contract(
-                hid[:, units], y_recv[:, :, :, cols].reshape(slots, dtile), 0, 0
+                hid[:, units], y_recv[:, :, :, cols].reshape(slots, wide), 0, 0
             ).astype(BF)
 
     def tokens_out():
@@ -509,33 +519,24 @@
                 contract(hi[...], back, 0, 0) + contract(low[...], back, 0, 0)
             ).astype(BF)
 
-        stores[0].start()
-
-    def tokens_dx():
-        b_wait(0)
-        b_wait(1)
+    def tokens_dx(p):
+        b_wait(p)
 
         @pl.loop(0, nd)
         def _(j):
             cols = pl.ds(pl.multiple_of(j * dtile, dtile), dtile)
-            back = b_recv[:, :, :, cols].reshape(slots, dtile)
-            dx_ref[:, cols] = contract(pick[...], back, 0, 0).astype(BF)
-
-        stores[1].start()
-
-    stores = [
-        pltpu.make_async_copy(src, dst, store_sem.at[i])
-        for i, (src, dst) in enumerate(
-            (
-                (out_ref, out_hbm),
-                (dx_ref, dx_hbm),
-                (gg_out, gg_hbm),
-                (gu_out, gu_hbm),
-                (gd_out, gd_hbm),
+            back = contract(
+                pick[p * n_rows : (p + 1) * n_rows, :],
+                b_recv[p, :, :, cols].reshape(n_rows, dtile),
+                0,
+                0,
             )
-        )
-    ]
-    cut1, cut2 = nf // 3, nf * 2 // 3
+            if p == 0:
+                dx_half[:, cols] = back
+            else:
+                dx_ref[:, cols] = (dx_half[:, cols] + back).astype(BF)
+
+    cut1 = nf // 3
 
     x_wait(0)
     hidden_units(0)
@@ -544,51 +545,41 @@
     o_start(0)
     hidden_units(1)
     gate_up(0, 1)
-    gate_up(1, 3)
+    down_units(0, cut1)
     ring_step(1, 0)
     ring_step(2, 0)
-    output_rows(1)
-    o_start(1)
-    down_units(0, cut1)
-    ring_step(1, 1)
-    down_units(cut1, cut2)
-    ring_step(2, 1)
-    down_units(cut2, nf)
+    down_units(cut1, nf)
 
     @pl.loop(0, n_z)
     def _(k):
         twin_copy(0, ring_order(k)).start()
 
+    gate_up(1, 3)
+    ring_step(0, 0)
+    output_rows(1)
+    o_start(1)
+    ring_step(1, 1)
+    ring_step(2, 1)
     gate_up(3, min(5, n_z))
-    ring_step(0, 0)
+    ring_step(0, 1)
+    input_rows(0, nd)
+    b_start(0)
+    b_start(1)
     if half > 2:
         ring_step(1, 2)
-    input_rows()
-    b_start(0)
-    b_start(1)
     if n_z > 5:
         gate_up(5, n_z)
     if half > 2:
         ring_step(2, 2)
-    ring_step(0, 1)
-    if half > 3:
-        ring_step(1, 3)
+        ring_step(0, 2)
     tokens_out()
-    if half > 2:
-        ring_step(0, 2)
-    if half > 3:
-        ring_step(2, 3)
-        ring_step(0, 3)
-    for s in range(4, half):
+    for s in range(3, half):
         for i in (1, 2, 0):
             ring_step(i, s)
-    tokens_dx()
+    tokens_dx(0)
+    tokens_dx(1)
     for i in (1, 2, 0):
         ring_last(i)
-        stores[(4, 2, 3)[i]].start()
-
-    for copy in stores:
-        copy.wait()
 
     for done in (meta_done, v_done, seq_done, x_done, y_done, o_done, b_done):
         done()
@@ -609,30 +600,24 @@
 
 
 def settle_kernel(*refs):
-    n = (len(refs) - 2) // 3
-    src, dst, held, sems = refs[:n], refs[n : 2 * n], refs[2 * n : 3 * n], refs[3 * n :]
-    ins = [pltpu.make_async_copy(src[i], held[i], sems[0].at[i]) for i in range(n)]
-    outs = [pltpu.make_async_copy(held[i], dst[i], sems[1].at[i]) for i in range(n)]
-    for copy in ins:
+    n = (len(refs) - 1) // 2
+    copies = [pltpu.make_async_copy(refs[i], refs[n + i], refs[2 * n].at[i]) for i in range(n)]
+    for copy in copies:
         copy.start()
-    for i in range(n):
-        ins[i].wait()
-        outs[i].start()
-    for copy in outs:
+    for copy in copies:
         copy.wait()
 
 
 def settle(arrays):
     n = len(arrays)
-    hbm = pl.BlockSpec(memory_space=pl.ANY)
     return pl.pallas_call(
         settle_kernel,
         out_shape=[jax.ShapeDtypeStruct(a.shape, a.dtype) for a in arrays],
-        in_specs=[hbm] * n,
-        out_specs=[hbm] * n,
-        scratch_shapes=[pltpu.VMEM(a.shape, a.dtype) for a in arrays]
-        + [pltpu.SemaphoreType.DMA((n,)), pltpu.SemaphoreType.DMA((n,))],
-    )(*arrays)
+        in_specs=[pl.BlockSpec(memory_space=pltpu.VMEM)] * n,
+        out_specs=[pl.BlockSpec(memory_space=pl.ANY)] * n,
+        scratch_shapes=[pltpu.SemaphoreType.DMA((n,))],
+        compiler_params=pltpu.CompilerParams(vmem_limit_bytes=4 * 1024 * 1024),
+    )(*[pltpu.with_memory_space_constraint(a, pltpu.VMEM) for a in arrays])
 
 
 def on_device(
@@ -669,20 +654,15 @@
     outs = pl.pallas_call(
         functools.partial(step_kernel, n_dp, n_ex, slot, cap),
         out_shape=(
-            jax.ShapeDtypeStruct((rows, width), BF),
-            jax.ShapeDtypeStruct((rows, width), BF),
-            jax.ShapeDtypeStruct((part, ff), BF),
-            jax.ShapeDtypeStruct((part, ff), BF),
-            jax.ShapeDtypeStruct((part_d, width), BF),
-        ),
-        in_specs=[vmem] * 5 + [hbm] * 5,
-        out_specs=[hbm] * 5,
-        scratch_shapes=[
             pltpu.VMEM((rows, width), BF),
             pltpu.VMEM((rows, width), BF),
             pltpu.VMEM((part, ff), BF),
             pltpu.VMEM((part, ff), BF),
             pltpu.VMEM((part_d, width), BF),
+        ),
+        in_specs=[vmem] * 5 + [hbm] * 5,
+        out_specs=[vmem] * 5,
+        scratch_shapes=[
             pltpu.VMEM((rows, width), BF),
             pltpu.VMEM((rows, width), BF),
             pltpu.VMEM((width, ff), BF),
@@ -698,16 +678,15 @@
             pltpu.VMEM((slots, rows), BF),
             pltpu.VMEM((slots, rows), BF),
             pltpu.VMEM((slots, rows), BF),
+            pltpu.VMEM((rows, width), F32),
             pltpu.VMEM((slots, ff), F32),
             pltpu.VMEM((slots, ff), BF),
-            pltpu.VMEM((slots, ff), BF),
-            pltpu.VMEM((slots, ff), BF),
+            pltpu.VMEM((slots, 2 * ff), BF),
             pltpu.VMEM((width, ff), BF),
             pltpu.VMEM((width, ff), BF),
             pltpu.VMEM((ff, width), BF),
             *twin,
             *ring,
-            dma((5,)),
             dma((5,)),
             dma((3,)),
             dma((1, 3)),
@@ -719,7 +698,7 @@
             dma((3, 2, n_z // 2)),
         ],
         compiler_params=pltpu.CompilerParams(
-            collective_id=0, has_side_effects=True, vmem_limit_bytes=67043328
+            collective_id=0, has_side_effects=True, vmem_limit_bytes=62 * 1024 * 1024
         ),
     )(
         destination[0],

time: 125 us -> 120 us (0.960)
  Pallas kernels: 122 us -> 117 us
    pallas_call x1, Pallas kernels: 120 us -> 116 us  [on_device(): pl.pallas_call(functools.partial(step_kernel, n_dp, n_ex, slot, cap), out...]
where the time goes in v4:
time: 120 us; the launch traced here: 118 us
  Pallas kernels  117 us (98%)
    pallas_call x1, Pallas kernels, on_device(): pl.pallas_call(functools.partial(step_kernel, n_dp, n_ex, slot, cap), out...  116 us

profile of v4, /device:TPU:1, one launch (start us, length us, event | category | flops | bytes accessed | tf_op | source)
XLA Modules:
  0.0 117.6 jit_solution(16186264853638443405)
XLA Ops:
  0.6 115.7 %shard_map.137 = (bf16[128,2048]{1,0:T(8,128)(2,1)S(1)}, bf16[128,2048]{1,0:T(8,128)(2,1)S(1)}, bf16[128,768]{1,0:T(8,128)(2,1)S(1)}, bf16[128,768]{1,0:T(8,128)(2,1)S(1)}, bf16[48,2048]{1,0:T(8,128)(2,1)S(1)}) custom-call(s32[1,8]{1,0:T(1,128)} %bitcast.16, s32[1,8]{1,0:T(1,128)} %bitcast.17, bf16[1,8]{1,0:T(2,128)(2,1)} %bitcast.18, s32[2,128]{1,0:T(2,128)} %bitcast.14, ...), custom_call_target="tpu_custom_call" | custom-call | tf_op jit(solution)/shard_map/pallas_call | solution.py:654
  116.4 1.2 %shard_map.138 = (bf16[128,2048]{1,0:T(8,128)(2,1)}, bf16[128,2048]{1,0:T(8,128)(2,1)}, bf16[128,768]{1,0:T(8,128)(2,1)}, bf16[128,768]{1,0:T(8,128)(2,1)}, bf16[48,2048]{1,0:T(8,128)(2,1)}) custom-call(bf16[128,2048]{1,0:T(8,128)(2,1)S(1)} %get-tuple-element.15.refs_0_, bf16[128,2048]{1,0:T(8,128)(2,1)S(1)} %get-tuple-element.16.refs_1_, ...), custom_call_target="tpu_custom_call" | custom-call | tf_op jit(solution)/shard_map/pallas_call | solution.py:613

commit v5 on v4

--- a/solution.py
+++ b/solution.py
@@ -66,6 +66,8 @@
     hi,
     low,
     dx_half,
+    gate_part,
+    up_part,
     hidden_grad,
     hid,
     both,
@@ -168,14 +170,18 @@
     spread = jnp.where(same_place, spread, 0.0).astype(BF)
     loads[0].wait()
 
-    @pl.loop(0, nd)
-    def _(j):
-        cols = pl.ds(pl.multiple_of(j * dtile, dtile), dtile)
-        seq_send[:, :, cols] = (
-            jnp.dot(spread, gen_ref[:, cols], preferred_element_type=F32)
-            .astype(BF)
-            .reshape(n_dp, slot, dtile)
-        )
+    mid = width // 2
+    for h in range(2):
+
+        @pl.loop(0, nd // 2)
+        def _(j):
+            cols = pl.ds(pl.multiple_of(j * dtile, dtile), dtile)
+            from_cols = pl.ds(pl.multiple_of(h * mid + j * dtile, dtile), dtile)
+            seq_send[h, :, :, cols] = (
+                jnp.dot(spread, gen_ref[:, from_cols], preferred_element_type=F32)
+                .astype(BF)
+                .reshape(n_dp, slot, dtile)
+            )
 
     def dp_exchange(send, recv, sems):
         def copy(src, dst, peer):
@@ -230,14 +236,23 @@
             copy(p, pl.ds(0, last)).wait_recv()
 
         def wait_send():
-            for p in range(send.shape[0]):
+            for p in range(sems.shape[0]):
                 copy(p, pl.ds(0, last)).wait_send()
 
         return start, wait_recv, wait_send
 
     meta_start, meta_wait, meta_done = dp_exchange(meta_send, meta_recv, meta_sem)
-    seq_start, seq_wait, seq_done = dp_exchange(seq_send, seq_recv, seq_sem)
-    x_start, x_wait, x_done = token_exchange(1, x_send, x_recv, x_sem)
+    seqs_of = [dp_exchange(seq_send.at[h], seq_recv.at[h], seq_sem.at[h]) for h in range(2)]
+    halves = [pl.ds(h * mid, mid) for h in range(2)]
+    x_of = [
+        token_exchange(
+            1,
+            x_send.at[:, :, :, halves[h]],
+            x_recv.at[:, :, :, halves[h]],
+            x_sem.at[h],
+        )
+        for h in range(2)
+    ]
     y_start, y_wait, y_done = token_exchange(1, y_send, y_recv, y_sem)
     v_start, v_wait, v_done = token_exchange(1, scale_send, scale_recv, scale_sem)
     o_start, o_wait, o_done = token_exchange(-1, o_send, o_recv, o_sem)
@@ -245,7 +260,8 @@
 
     pl.semaphore_wait(barrier, n_dp + n_ex - 2)
     meta_start()
-    seq_start()
+    for seq_start, _, _ in seqs_of:
+        seq_start()
 
     names = jnp.zeros((n_ex, rows), jnp.int32)
     for i in range(n_ex):
@@ -310,21 +326,26 @@
     scale_send[0] = jnp.broadcast_to(spread_scale, (n_ex, 8, lanes))
     v_start(0)
     fetch = contract(picked, placed.astype(BF), 1, 1).astype(BF)
-    seq_wait()
-
-    for p in range(2):
-
-        @pl.loop(0, nd)
+    def fill_x(h, p):
+        here = slice(p * n_rows, (p + 1) * n_rows)
+
+        @pl.loop(0, nd // 2)
         def _(j):
             cols = pl.ds(pl.multiple_of(j * dtile, dtile), dtile)
-            source = seq_recv[:, :, cols].reshape(n_dp * slot, dtile)
-            x_send[p, :, :, cols] = (
-                jnp.dot(fetch[p * n_rows : (p + 1) * n_rows, :], source, preferred_element_type=F32)
+            to_cols = pl.ds(pl.multiple_of(h * mid + j * dtile, dtile), dtile)
+            source = seq_recv[h, :, :, cols].reshape(n_dp * slot, dtile)
+            x_send[p, :, :, to_cols] = (
+                jnp.dot(fetch[here, :], source, preferred_element_type=F32)
                 .astype(BF)
                 .reshape(n_ex, hc, dtile)
             )
 
-        x_start(p)
+        x_of[h][0](p)
+
+    for h in range(2):
+        seqs_of[h][1]()
+        fill_x(h, 0)
+        fill_x(h, 1)
 
     y_wait(0)
     y_wait(1)
@@ -350,15 +371,30 @@
         cols = pl.ds(pl.multiple_of(j * ftile, ftile), ftile)
         hidden_grad[:, cols] = contract(y_recv[...].reshape(slots, width), wd[cols, :], 1, 1)
 
+    def first_products():
+        x_of[0][1](0)
+        x_of[0][1](1)
+
+        @pl.loop(0, nf)
+        def _(j):
+            cols = pl.ds(pl.multiple_of(j * ftile, ftile), ftile)
+            x_some = x_recv[:, :, :, :mid].reshape(slots, mid)
+            gate_part[:, cols] = jnp.dot(x_some, wg[:mid, cols], preferred_element_type=F32)
+            up_part[:, cols] = jnp.dot(x_some, wu[:mid, cols], preferred_element_type=F32)
+
     def hidden_units(p):
         here = pl.ds(p * n_rows, n_rows)
 
         @pl.loop(0, nf)
         def _(j):
             cols = pl.ds(pl.multiple_of(j * ftile, ftile), ftile)
-            x_some = x_recv[p].reshape(n_rows, width)
-            gate_pre = jnp.dot(x_some, wg[:, cols], preferred_element_type=F32)
-            up_pre = jnp.dot(x_some, wu[:, cols], preferred_element_type=F32)
+            x_some = x_recv[p, :, :, mid:].reshape(n_rows, mid)
+            gate_pre = gate_part[here, cols] + jnp.dot(
+                x_some, wg[mid:, cols], preferred_element_type=F32
+            )
+            up_pre = up_part[here, cols] + jnp.dot(
+                x_some, wu[mid:, cols], preferred_element_type=F32
+            )
             sig = jax.nn.sigmoid(gate_pre)
             act = gate_pre * sig
             hid[here, cols] = (act * up_pre).astype(BF)
@@ -538,10 +574,11 @@
 
     cut1 = nf // 3
 
-    x_wait(0)
+    first_products()
+    x_of[1][1](0)
     hidden_units(0)
     output_rows(0)
-    x_wait(1)
+    x_of[1][1](1)
     o_start(0)
     hidden_units(1)
     gate_up(0, 1)
@@ -581,7 +618,17 @@
     for i in (1, 2, 0):
         ring_last(i)
 
-    for done in (meta_done, v_done, seq_done, x_done, y_done, o_done, b_done):
+    for done in (
+        meta_done,
+        v_done,
+        seqs_of[0][2],
+        seqs_of[1][2],
+        x_of[0][2],
+        x_of[1][2],
+        y_done,
+        o_done,
+        b_done,
+    ):
         done()
 
     for i in range(3):
@@ -672,13 +719,15 @@
             pltpu.VMEM((n_dp, 8, 128), F32),
             pltpu.VMEM((1, n_ex, 8, lanes), F32),
             pltpu.VMEM((1, n_ex, 8, lanes), F32),
-            pltpu.VMEM((n_dp, slot, width), BF),
-            pltpu.VMEM((n_dp, slot, width), BF),
+            pltpu.VMEM((2, n_dp, slot, width // 2), BF),
+            pltpu.VMEM((2, n_dp, slot, width // 2), BF),
             *buffers,
             pltpu.VMEM((slots, rows), BF),
             pltpu.VMEM((slots, rows), BF),
             pltpu.VMEM((slots, rows), BF),
             pltpu.VMEM((rows, width), F32),
+            pltpu.VMEM((slots, ff), F32),
+            pltpu.VMEM((slots, ff), F32),
             pltpu.VMEM((slots, ff), F32),
             pltpu.VMEM((slots, ff), BF),
             pltpu.VMEM((slots, 2 * ff), BF),
@@ -690,8 +739,9 @@
             dma((5,)),
             dma((3,)),
             dma((1, 3)),
-            dma((3,)),
-            *([dma((2, 3))] * 4),
+            dma((2, 3)),
+            dma((2, 2, 3)),
+            *([dma((2, 3))] * 3),
             dma((3,)),
             dma((3, n_z)),
             dma((3,)),

time: 120 us -> 116 us (0.967); the launches traced: 118 us -> 116 us
  Pallas kernels: 117 us -> 115 us
    pallas_call x1, Pallas kernels: 116 us -> 114 us  [on_device(): pl.pallas_call(functools.partial(step_kernel, n_dp, n_ex, slot, cap), out...]
where the time goes in v5:
time: 116 us
  Pallas kernels  115 us (99%)
    pallas_call x1, Pallas kernels, on_device(): pl.pallas_call(functools.partial(step_kernel, n_dp, n_ex, slot, cap), out...  114 us

profile of v5, /device:TPU:1, one launch (start us, length us, event | category | flops | bytes accessed | tf_op | source)
XLA Modules:
  0.0 115.7 jit_solution(2785144476850793732)
XLA Ops:
  0.6 113.9 %shard_map.137 = (bf16[128,2048]{1,0:T(8,128)(2,1)S(1)}, bf16[128,2048]{1,0:T(8,128)(2,1)S(1)}, bf16[128,768]{1,0:T(8,128)(2,1)S(1)}, bf16[128,768]{1,0:T(8,128)(2,1)S(1)}, bf16[48,2048]{1,0:T(8,128)(2,1)S(1)}) custom-call(s32[1,8]{1,0:T(1,128)} %bitcast.16, s32[1,8]{1,0:T(1,128)} %bitcast.17, bf16[1,8]{1,0:T(2,128)(2,1)} %bitcast.18, s32[2,128]{1,0:T(2,128)} %bitcast.14, ...), custom_call_target="tpu_custom_call" | custom-call | tf_op jit(solution)/shard_map/pallas_call | solution.py:701
  114.5 1.2 %shard_map.138 = (bf16[128,2048]{1,0:T(8,128)(2,1)}, bf16[128,2048]{1,0:T(8,128)(2,1)}, bf16[128,768]{1,0:T(8,128)(2,1)}, bf16[128,768]{1,0:T(8,128)(2,1)}, bf16[48,2048]{1,0:T(8,128)(2,1)}) custom-call(bf16[128,2048]{1,0:T(8,128)(2,1)S(1)} %get-tuple-element.15.refs_0_, bf16[128,2048]{1,0:T(8,128)(2,1)S(1)} %get-tuple-element.16.refs_1_, ...), custom_call_target="tpu_custom_call" | custom-call | tf_op jit(solution)/shard_map/pallas_call | solution.py:660

commit v6 on v5

--- a/solution.py
+++ b/solution.py
@@ -102,6 +102,7 @@
     rows = gen_ref.shape[0]
     width = gen_ref.shape[1]
     ff = wg.shape[1]
+    mid = width // 2
     slots = n_ex * cap
     hc = cap // 2
     lanes = max(cap, 128)
@@ -134,6 +135,15 @@
         dz, dc = trainers[i]
         return lax.rem(z + dz, n_z) * 2 + lax.rem(core + dc, 2)
 
+    loads = [
+        pltpu.make_async_copy(src, dst, w_sem.at[i])
+        for i, (src, dst) in enumerate(
+            ((cot_hbm, cot_ref), (gen_hbm, gen_ref), (wg_hbm, wg), (wu_hbm, wu), (wd_hbm, wd))
+        )
+    ]
+    for copy in loads:
+        copy.start()
+
     barrier = pltpu.get_barrier_semaphore()
 
     @pl.loop(1, n_dp)
@@ -145,43 +155,6 @@
         pl.semaphore_signal(
             barrier, 1, device_id={"expert": lax.rem(e + o, n_ex)}, device_id_type=MESH
         )
-
-    loads = [
-        pltpu.make_async_copy(src, dst, w_sem.at[i])
-        for i, (src, dst) in enumerate(
-            ((gen_hbm, gen_ref), (cot_hbm, cot_ref), (wg_hbm, wg), (wu_hbm, wu), (wd_hbm, wd))
-        )
-    ]
-    for copy in loads:
-        copy.start()
-
-    shift = slot.bit_length() - 1
-    seqs = dest_ref.shape[1]
-    srow, scol = iota((n_dp * slot, rows), 0), iota((n_dp * slot, rows), 1)
-    same_place = (srow & (slot - 1)) == (scol & (slot - 1))
-    mine = dest_ref[...] == iota((n_dp, seqs), 0)
-    len_to = jnp.sum(jnp.where(mine, len_ref[...].astype(F32), 0.0), axis=1, keepdims=True)
-    adv_to = jnp.sum(jnp.where(mine, adv_ref[...].astype(F32), 0.0), axis=1, keepdims=True)
-    line = iota((n_dp, 8, 128), 1)
-    meta_send[...] = jnp.where(line == 0, len_to[:, :, None], adv_to[:, :, None])
-    seq_lanes = ((iota((seqs, rows), 1) >> shift) == iota((seqs, rows), 0)).astype(F32)
-    mine_lanes = jnp.dot(mine.astype(F32), seq_lanes, preferred_element_type=F32)
-    spread = jnp.broadcast_to(mine_lanes[:, None, :], (n_dp, slot, rows)).reshape(n_dp * slot, rows)
-    spread = jnp.where(same_place, spread, 0.0).astype(BF)
-    loads[0].wait()
-
-    mid = width // 2
-    for h in range(2):
-
-        @pl.loop(0, nd // 2)
-        def _(j):
-            cols = pl.ds(pl.multiple_of(j * dtile, dtile), dtile)
-            from_cols = pl.ds(pl.multiple_of(h * mid + j * dtile, dtile), dtile)
-            seq_send[h, :, :, cols] = (
-                jnp.dot(spread, gen_ref[:, from_cols], preferred_element_type=F32)
-                .astype(BF)
-                .reshape(n_dp, slot, dtile)
-            )
 
     def dp_exchange(send, recv, sems):
         def copy(src, dst, peer):
@@ -257,11 +230,6 @@
     v_start, v_wait, v_done = token_exchange(1, scale_send, scale_recv, scale_sem)
     o_start, o_wait, o_done = token_exchange(-1, o_send, o_recv, o_sem)
     b_start, b_wait, b_done = token_exchange(-1, b_send, b_recv, b_sem)
-
-    pl.semaphore_wait(barrier, n_dp + n_ex - 2)
-    meta_start()
-    for seq_start, _, _ in seqs_of:
-        seq_start()
 
     names = jnp.zeros((n_ex, rows), jnp.int32)
     for i in range(n_ex):
@@ -281,23 +249,59 @@
     hi[...] = whole
     low[...] = (weighted - whole.astype(F32)).astype(BF)
 
-    loads[1].wait()
-
     n_rows = n_ex * hc
 
-    for p in range(2):
-
+    def fill_y(p):
         @pl.loop(0, nd)
         def _(j):
             cols = pl.ds(pl.multiple_of(j * dtile, dtile), dtile)
             y_send[p, :, :, cols] = (
-                jnp.dot(pick[p * n_rows : (p + 1) * n_rows, :], cot_ref[:, cols], preferred_element_type=F32)
+                jnp.dot(
+                    pick[p * n_rows : (p + 1) * n_rows, :],
+                    cot_ref[:, cols],
+                    preferred_element_type=F32,
+                )
                 .astype(BF)
                 .reshape(n_ex, hc, dtile)
             )
 
-        y_start(p)
-
+    loads[0].wait()
+    fill_y(0)
+    pl.semaphore_wait(barrier, n_dp + n_ex - 2)
+    y_start(0)
+
+    shift = slot.bit_length() - 1
+    seqs = dest_ref.shape[1]
+    srow, scol = iota((n_dp * slot, rows), 0), iota((n_dp * slot, rows), 1)
+    same_place = (srow & (slot - 1)) == (scol & (slot - 1))
+    mine = dest_ref[...] == iota((n_dp, seqs), 0)
+    len_to = jnp.sum(jnp.where(mine, len_ref[...].astype(F32), 0.0), axis=1, keepdims=True)
+    adv_to = jnp.sum(jnp.where(mine, adv_ref[...].astype(F32), 0.0), axis=1, keepdims=True)
+    line = iota((n_dp, 8, 128), 1)
+    meta_send[...] = jnp.where(line == 0, len_to[:, :, None], adv_to[:, :, None])
+    seq_lanes = ((iota((seqs, rows), 1) >> shift) == iota((seqs, rows), 0)).astype(F32)
+    mine_lanes = jnp.dot(mine.astype(F32), seq_lanes, preferred_element_type=F32)
+    spread = jnp.broadcast_to(mine_lanes[:, None, :], (n_dp, slot, rows)).reshape(n_dp * slot, rows)
+    spread = jnp.where(same_place, spread, 0.0).astype(BF)
+    meta_start()
+    loads[1].wait()
+
+    for h in range(2):
+
+        @pl.loop(0, nd // 2)
+        def _(j):
+            cols = pl.ds(pl.multiple_of(j * dtile, dtile), dtile)
+            from_cols = pl.ds(pl.multiple_of(h * mid + j * dtile, dtile), dtile)
+            seq_send[h, :, :, cols] = (
+                jnp.dot(spread, gen_ref[:, from_cols], preferred_element_type=F32)
+                .astype(BF)
+                .reshape(n_dp, slot, dtile)
+            )
+
+        seqs_of[h][0]()
+
+    fill_y(1)
+    y_start(1)
     meta_wait()
 
     got_len = meta_recv[:, 0, :]
@@ -609,10 +613,10 @@
     if half > 2:
         ring_step(2, 2)
         ring_step(0, 2)
-    tokens_out()
     for s in range(3, half):
         for i in (1, 2, 0):
             ring_step(i, s)
+    tokens_out()
     tokens_dx(0)
     tokens_dx(1)
     for i in (1, 2, 0):

time: 116 us -> 114 us (0.983)
  Pallas kernels: 115 us -> 113 us
    pallas_call x1, Pallas kernels: 114 us -> 112 us  [on_device(): pl.pallas_call(functools.partial(step_kernel, n_dp, n_ex, slot, cap), out...]
where the time goes in v6:
time: 114 us
  Pallas kernels  113 us (99%)
    pallas_call x1, Pallas kernels, on_device(): pl.pallas_call(functools.partial(step_kernel, n_dp, n_ex, slot, cap), out...  112 us

profile of v6, /device:TPU:1, one launch (start us, length us, event | category | flops | bytes accessed | tf_op | source)
XLA Modules:
  0.0 113.7 jit_solution(7253913348247486556)
XLA Ops:
  0.6 111.9 %shard_map.137 = (bf16[128,2048]{1,0:T(8,128)(2,1)S(1)}, bf16[128,2048]{1,0:T(8,128)(2,1)S(1)}, bf16[128,768]{1,0:T(8,128)(2,1)S(1)}, bf16[128,768]{1,0:T(8,128)(2,1)S(1)}, bf16[48,2048]{1,0:T(8,128)(2,1)S(1)}) custom-call(s32[1,8]{1,0:T(1,128)} %bitcast.16, s32[1,8]{1,0:T(1,128)} %bitcast.17, bf16[1,8]{1,0:T(2,128)(2,1)} %bitcast.18, s32[2,128]{1,0:T(2,128)} %bitcast.14, ...), custom_call_target="tpu_custom_call" | custom-call | tf_op jit(solution)/shard_map/pallas_call | solution.py:705
  112.5 1.2 %shard_map.138 = (bf16[128,2048]{1,0:T(8,128)(2,1)}, bf16[128,2048]{1,0:T(8,128)(2,1)}, bf16[128,768]{1,0:T(8,128)(2,1)}, bf16[128,768]{1,0:T(8,128)(2,1)}, bf16[48,2048]{1,0:T(8,128)(2,1)}) custom-call(bf16[128,2048]{1,0:T(8,128)(2,1)S(1)} %get-tuple-element.15.refs_0_, bf16[128,2048]{1,0:T(8,128)(2,1)S(1)} %get-tuple-element.16.refs_1_, ...), custom_call_target="tpu_custom_call" | custom-call | tf_op jit(solution)/shard_map/pallas_call | solution.py:664

commit v7 on v6

--- a/solution.py
+++ b/solution.py
@@ -146,15 +146,15 @@
 
     barrier = pltpu.get_barrier_semaphore()
 
-    @pl.loop(1, n_dp)
-    def _(o):
-        pl.semaphore_signal(barrier, 1, device_id={"dp": lax.rem(g + o, n_dp)}, device_id_type=MESH)
-
-    @pl.loop(1, n_ex)
-    def _(o):
-        pl.semaphore_signal(
-            barrier, 1, device_id={"expert": lax.rem(e + o, n_ex)}, device_id_type=MESH
-        )
+    for i in range(max(n_dp, n_ex) - 1):
+        if i < n_dp - 1:
+            pl.semaphore_signal(
+                barrier, 1, device_id={"dp": trainer_to(i)}, device_id_type=MESH
+            )
+        if i < n_ex - 1:
+            pl.semaphore_signal(
+                barrier, 1, device_id={"expert": expert_to(i)}, device_id_type=MESH
+            )
 
     def dp_exchange(send, recv, sems):
         def copy(src, dst, peer):
@@ -252,7 +252,7 @@
     n_rows = n_ex * hc
 
     def fill_y(p):
-        @pl.loop(0, nd)
+        @pl.loop(0, nd, unroll=4)
         def _(j):
             cols = pl.ds(pl.multiple_of(j * dtile, dtile), dtile)
             y_send[p, :, :, cols] = (
@@ -389,7 +389,7 @@
     def hidden_units(p):
         here = pl.ds(p * n_rows, n_rows)
 
-        @pl.loop(0, nf)
+        @pl.loop(0, nf, unroll=True)
         def _(j):
             cols = pl.ds(pl.multiple_of(j * ftile, ftile), ftile)
             x_some = x_recv[p, :, :, mid:].reshape(n_rows, mid)
@@ -562,7 +562,7 @@
     def tokens_dx(p):
         b_wait(p)
 
-        @pl.loop(0, nd)
+        @pl.loop(0, nd, unroll=2)
         def _(j):
             cols = pl.ds(pl.multiple_of(j * dtile, dtile), dtile)
             back = contract(
@@ -587,6 +587,7 @@
     hidden_units(1)
     gate_up(0, 1)
     down_units(0, cut1)
+    gate_up(1, 2)
     ring_step(1, 0)
     ring_step(2, 0)
     down_units(cut1, nf)
@@ -595,7 +596,7 @@
     def _(k):
         twin_copy(0, ring_order(k)).start()
 
-    gate_up(1, 3)
+    gate_up(2, 3)
     ring_step(0, 0)
     output_rows(1)
     o_start(1)

time: 114 us -> 113 us (level)
  Pallas kernels: 113 us -> 111 us
    pallas_call x1, Pallas kernels: 112 us -> 110 us  [on_device(): pl.pallas_call(functools.partial(step_kernel, n_dp, n_ex, slot, cap), out...]
where the time goes in v7:
time: 113 us; the launch traced here: 112 us
  Pallas kernels  111 us (98%)
    pallas_call x1, Pallas kernels, on_device(): pl.pallas_call(functools.partial(step_kernel, n_dp, n_ex, slot, cap), out...  110 us

profile of v7, /device:TPU:1, one launch (start us, length us, event | category | flops | bytes accessed | tf_op | source)
XLA Modules:
  0.0 112.1 jit_solution(8528742234977123638)
XLA Ops:
  0.6 110.3 %shard_map.137 = (bf16[128,2048]{1,0:T(8,128)(2,1)S(1)}, bf16[128,2048]{1,0:T(8,128)(2,1)S(1)}, bf16[128,768]{1,0:T(8,128)(2,1)S(1)}, bf16[128,768]{1,0:T(8,128)(2,1)S(1)}, bf16[48,2048]{1,0:T(8,128)(2,1)S(1)}) custom-call(s32[1,8]{1,0:T(1,128)} %bitcast.16, s32[1,8]{1,0:T(1,128)} %bitcast.17, bf16[1,8]{1,0:T(2,128)(2,1)} %bitcast.18, s32[2,128]{1,0:T(2,128)} %bitcast.14, ...), custom_call_target="tpu_custom_call" | custom-call | tf_op jit(solution)/shard_map/pallas_call | solution.py:706
  110.9 1.2 %shard_map.138 = (bf16[128,2048]{1,0:T(8,128)(2,1)}, bf16[128,2048]{1,0:T(8,128)(2,1)}, bf16[128,768]{1,0:T(8,128)(2,1)}, bf16[128,768]{1,0:T(8,128)(2,1)}, bf16[48,2048]{1,0:T(8,128)(2,1)}) custom-call(bf16[128,2048]{1,0:T(8,128)(2,1)S(1)} %get-tuple-element.15.refs_0_, bf16[128,2048]{1,0:T(8,128)(2,1)S(1)} %get-tuple-element.16.refs_1_, ...), custom_call_target="tpu_custom_call" | custom-call | tf_op jit(solution)/shard_map/pallas_call | solution.py:665

commit v8 on v7

--- a/solution.py
+++ b/solution.py
@@ -333,7 +333,7 @@
     def fill_x(h, p):
         here = slice(p * n_rows, (p + 1) * n_rows)
 
-        @pl.loop(0, nd // 2)
+        @pl.loop(0, nd // 2, unroll=2)
         def _(j):
             cols = pl.ds(pl.multiple_of(j * dtile, dtile), dtile)
             to_cols = pl.ds(pl.multiple_of(h * mid + j * dtile, dtile), dtile)
@@ -379,7 +379,7 @@
         x_of[0][1](0)
         x_of[0][1](1)
 
-        @pl.loop(0, nf)
+        @pl.loop(0, nf, unroll=True)
         def _(j):
             cols = pl.ds(pl.multiple_of(j * ftile, ftile), ftile)
             x_some = x_recv[:, :, :, :mid].reshape(slots, mid)
@@ -412,7 +412,7 @@
     def output_rows(p):
         here = pl.ds(p * n_rows, n_rows)
 
-        @pl.loop(0, nd)
+        @pl.loop(0, nd, unroll=4)
         def _(j):
             cols = pl.ds(pl.multiple_of(j * dtile, dtile), dtile)
             o_send[p, :, :, cols] = (
@@ -422,7 +422,7 @@
             )
 
     def input_rows(lo, hi):
-        @pl.loop(lo, hi)
+        @pl.loop(lo, hi, unroll=2)
         def _(j):
             cols = pl.ds(pl.multiple_of(j * dtile, dtile), dtile)
             b_send[:, :, :, cols] = (
@@ -551,7 +551,7 @@
         o_wait(0)
         o_wait(1)
 
-        @pl.loop(0, nd)
+        @pl.loop(0, nd, unroll=2)
         def _(j):
             cols = pl.ds(pl.multiple_of(j * dtile, dtile), dtile)
             back = o_recv[:, :, :, cols].reshape(slots, dtile)

time: 113 us -> 112 us (level)
  no operation moved by 1% of the time
where the time goes in v8:
time: 112 us
  Pallas kernels  111 us (99%)
    pallas_call x1, Pallas kernels, on_device(): pl.pallas_call(functools.partial(step_kernel, n_dp, n_ex, slot, cap), out...  110 us

profile of v8, /device:TPU:1, one launch (start us, length us, event | category | flops | bytes accessed | tf_op | source)
XLA Modules:
  0.0 111.6 jit_solution(15872883111291141791)
XLA Ops:
  0.6 109.7 %shard_map.137 = (bf16[128,2048]{1,0:T(8,128)(2,1)S(1)}, bf16[128,2048]{1,0:T(8,128)(2,1)S(1)}, bf16[128,768]{1,0:T(8,128)(2,1)S(1)}, bf16[128,768]{1,0:T(8,128)(2,1)S(1)}, bf16[48,2048]{1,0:T(8,128)(2,1)S(1)}) custom-call(s32[1,8]{1,0:T(1,128)} %bitcast.16, s32[1,8]{1,0:T(1,128)} %bitcast.17, bf16[1,8]{1,0:T(2,128)(2,1)} %bitcast.18, s32[2,128]{1,0:T(2,128)} %bitcast.14, ...), custom_call_target="tpu_custom_call" | custom-call | tf_op jit(solution)/shard_map/pallas_call | solution.py:706
  110.4 1.2 %shard_map.138 = (bf16[128,2048]{1,0:T(8,128)(2,1)}, bf16[128,2048]{1,0:T(8,128)(2,1)}, bf16[128,768]{1,0:T(8,128)(2,1)}, bf16[128,768]{1,0:T(8,128)(2,1)}, bf16[48,2048]{1,0:T(8,128)(2,1)}) custom-call(bf16[128,2048]{1,0:T(8,128)(2,1)S(1)} %get-tuple-element.15.refs_0_, bf16[128,2048]{1,0:T(8,128)(2,1)S(1)} %get-tuple-element.16.refs_1_, ...), custom_call_target="tpu_custom_call" | custom-call | tf_op jit(solution)/shard_map/pallas_call | solution.py:665

commit v9 on v8

--- a/solution.py
+++ b/solution.py
@@ -370,7 +370,7 @@
     for copy in loads[2:]:
         copy.wait()
 
-    @pl.loop(0, nf)
+    @pl.loop(0, nf, unroll=True)
     def _(j):
         cols = pl.ds(pl.multiple_of(j * ftile, ftile), ftile)
         hidden_grad[:, cols] = contract(y_recv[...].reshape(slots, width), wd[cols, :], 1, 1)
@@ -539,7 +539,7 @@
     def down_units(lo, hi):
         per = width // wide
 
-        @pl.loop(lo * per, hi * per)
+        @pl.loop(lo * per, hi * per, unroll=2)
         def _(j):
             units = pl.ds(pl.multiple_of(lax.div(j, per) * ftile, ftile), ftile)
             cols = pl.ds(pl.multiple_of(lax.rem(j, per) * wide, wide), wide)

time: 112 us -> 112 us (level)
  no operation moved by 1% of the time
where the time goes in v9:
time: 112 us
  Pallas kernels  111 us (99%)
    pallas_call x1, Pallas kernels, on_device(): pl.pallas_call(functools.partial(step_kernel, n_dp, n_ex, slot, cap), out...  110 us

profile of v9, /device:TPU:1, one launch (start us, length us, event | category | flops | bytes accessed | tf_op | source)
XLA Modules:
  0.0 111.9 jit_solution(759558171402803346)
XLA Ops:
  0.6 109.9 %shard_map.137 = (bf16[128,2048]{1,0:T(8,128)(2,1)S(1)}, bf16[128,2048]{1,0:T(8,128)(2,1)S(1)}, bf16[128,768]{1,0:T(8,128)(2,1)S(1)}, bf16[128,768]{1,0:T(8,128)(2,1)S(1)}, bf16[48,2048]{1,0:T(8,128)(2,1)S(1)}) custom-call(s32[1,8]{1,0:T(1,128)} %bitcast.16, s32[1,8]{1,0:T(1,128)} %bitcast.17, bf16[1,8]{1,0:T(2,128)(2,1)} %bitcast.18, s32[2,128]{1,0:T(2,128)} %bitcast.14, ...), custom_call_target="tpu_custom_call" | custom-call | tf_op jit(solution)/shard_map/pallas_call | solution.py:706
  110.5 1.2 %shard_map.138 = (bf16[128,2048]{1,0:T(8,128)(2,1)}, bf16[128,2048]{1,0:T(8,128)(2,1)}, bf16[128,768]{1,0:T(8,128)(2,1)}, bf16[128,768]{1,0:T(8,128)(2,1)}, bf16[48,2048]{1,0:T(8,128)(2,1)}) custom-call(bf16[128,2048]{1,0:T(8,128)(2,1)S(1)} %get-tuple-element.15.refs_0_, bf16[128,2048]{1,0:T(8,128)(2,1)S(1)} %get-tuple-element.16.refs_1_, ...), custom_call_target="tpu_custom_call" | custom-call | tf_op jit(solution)/shard_map/pallas_call | solution.py:665
